TPU v7x, 256 devices: a whole 4x4x8 slice. The times are simulated.
256 devices in a mesh: dp: 16 (over z, core), fsdp: 16 (over y, x).
Axes of the slice: x: 4, y: 4, z: 8, core: 2. Of those that a mesh axis runs over, the one named last changes fastest.
Arguments:
- hidden_in: bfloat16 [2048, 2304], P(('dp', 'fsdp')), may hold values from -30 to 30
- cache_pool: bfloat16 [8448, 16, 2, 2048], P('dp', None, None, 'fsdp'), may hold values from -64 to 64
- project_in: bfloat16 [2304, 3, 2048], P('dp', None, 'fsdp'), may hold values from -0.125 to 0.125
- project_out: bfloat16 [2048, 2304], P('fsdp', 'dp'), may hold values from -0.125 to 0.125
- norm_first: bfloat16 [2304], replicated, may hold values from 0.099609375 to 1.8984375
- norm_second: bfloat16 [2304], replicated, may hold values from 0.099609375 to 1.8984375
- router: bfloat16 [2304, 8], replicated, may hold values from -0.125 to 0.125
- gate_up: bfloat16 [8, 2304, 2, 5760], P(None, 'dp', None, 'fsdp'), may hold values from -0.125 to 0.125
- expert_down: bfloat16 [8, 2304, 5760], P(None, 'dp', 'fsdp'), may hold values from -0.078125 to 0.078125
- lengths: int32 [2048], replicated, may hold values from 65 to 128, as said below
- prompt_pages: int32 [64, 4], P('dp'), may hold values from 0 to 527, as said below
- own_pages: int32 [2048, 4], P('dp'), may hold values from 0 to 527, as said below
- groups: int32 [2048], P('dp'), may hold values from 0 to 3
- move_target: int32 [16, 8], replicated, may hold values from 0 to 15, as said below
- routes: int32 [2048, 2], P(('dp', 'fsdp')), may hold values from 0 to 7, all different within a row; in each aligned block of 8 rows (0 to 7, 8 to 15, ...) at most 4 rows name the same one
Outputs:
- layer_out: bfloat16 [2048, 2304], P(('dp', 'fsdp'))
Inputs may be any that keep to these rules, and one draw needn't show every extreme that they name: `lengths`: every request's cache holds its shared prompt's 4 * 16 positions and at least one more; some request holds 128. `prompt_pages`: within a row, the prompt pages of all its shared prompts and the own pages of all its requests are distinct pages. `own_pages`: within a row, the prompt pages of all its shared prompts and the own pages of all its requests are distinct pages. Row s sends its request slots 128 - 8 + j, j < 8, to rows move_target[s, j]; a row's 8 destinations are distinct and differ from s, and for each j every row is the destination of exactly one row. `routes`: in the 8 rows of one device no expert is named more than 4 times.
All inputs are finite; a program needn't handle non-finite values.
Results may differ from a plain program's by a relative error of at most 0.009.
Values may be sent and summed in bfloat16 or wider, within the bound.
A program may use at most 128 MiB of HBM per device.

v0:
```python
import jax
import jax.numpy as jnp
from jax import lax
from jax.sharding import PartitionSpec as P

HD = 64
CAP = 4


def rms_scale(values, scaling):
    return (
        values
        * lax.rsqrt(jnp.mean(values * values, axis=-1, keepdims=True) + 1e-06)
        * scaling.astype(jnp.float32)
    )


def rotate(tensor, position):
    half_dim = tensor.shape[-1] // 2
    channel = jnp.arange(half_dim, dtype=jnp.float32)
    inverse = jnp.exp(-jnp.log(10000.0) * 2.0 * channel / tensor.shape[-1])
    angles = position.astype(jnp.float32)[:, None, None] * inverse
    cosine = jnp.cos(angles)
    sine_part = jnp.sin(angles)
    first_half = tensor[..., :half_dim]
    second_half = tensor[..., half_dim:]
    return jnp.concatenate(
        [
            first_half * cosine - second_half * sine_part,
            second_half * cosine + first_half * sine_part,
        ],
        axis=-1,
    )


def local(
    hidden_in,
    cache_pool,
    project_in,
    project_out,
    norm_first,
    norm_second,
    router,
    gate_up,
    expert_down,
    lengths,
    prompt_pages,
    own_pages,
    groups,
    move_target,
    routes,
):
    rows_count = lax.axis_size("dp")
    fsdp_count = lax.axis_size("fsdp")
    my_row = lax.axis_index("dp")
    my_column = lax.axis_index("fsdp")
    req_local = hidden_in.shape[0]
    model_width = hidden_in.shape[1]
    req_row = req_local * fsdp_count
    movers = move_target.shape[1]
    staying = req_row - movers
    page_len = cache_pool.shape[1]
    head_cols = cache_pool.shape[3]
    heads_here = head_cols // HD
    span_total = (prompt_pages.shape[1] + own_pages.shape[1]) * page_len
    expert_count = router.shape[1]
    rows_per_expert = rows_count // expert_count
    slots_row = (CAP + rows_per_expert - 1) // rows_per_expert
    gate_send = jnp.repeat(gate_up, rows_per_expert, axis=0)
    down_send = jnp.repeat(expert_down, rows_per_expert, axis=0)
    row_tokens = lax.all_gather(hidden_in, "fsdp", axis=0, tiled=True)
    group_hit = (
        groups[:, None] == jnp.arange(prompt_pages.shape[0], dtype=jnp.int32)[None, :]
    ).astype(jnp.int32)
    prompt_list = jnp.sum(group_hit[:, :, None] * prompt_pages[None, :, :], axis=1)
    page_list = jnp.concatenate([prompt_list, own_pages], axis=1)
    mover_cache = cache_pool[page_list[staying:]]
    my_targets = move_target[my_row]
    send_select = (my_targets[:, None] == jnp.arange(rows_count, dtype=jnp.int32)[None, :]).astype(
        jnp.bfloat16
    )
    cache_send = jnp.einsum(
        "jd,jpqkc->dpqkc", send_select, mover_cache, preferred_element_type=jnp.float32
    ).astype(jnp.bfloat16)
    tokens_send = jnp.einsum(
        "jd,jc->dc", send_select, row_tokens[staying:], preferred_element_type=jnp.float32
    ).astype(jnp.bfloat16)
    cache_recv, tokens_recv = (
        lax.all_to_all(cache_send, "dp", split_axis=0, concat_axis=0, tiled=True),
        lax.all_to_all(tokens_send, "dp", split_axis=0, concat_axis=0, tiled=True),
    )
    arrive_hit = move_target == my_row
    arrive_select = arrive_hit.astype(jnp.bfloat16)
    arrived_cache = jnp.einsum(
        "sj,spqkc->jpqkc", arrive_select, cache_recv, preferred_element_type=jnp.float32
    ).astype(jnp.bfloat16)
    arrived_tokens = jnp.einsum(
        "sj,sc->jc", arrive_select, tokens_recv, preferred_element_type=jnp.float32
    ).astype(jnp.bfloat16)
    source_row = jnp.sum(
        arrive_hit.astype(jnp.int32) * jnp.arange(rows_count, dtype=jnp.int32)[:, None], axis=0
    )
    row_lengths = lax.dynamic_slice_in_dim(lengths, my_row * req_row, req_row)
    arrived_lengths = lengths[source_row * req_row + staying + jnp.arange(movers, dtype=jnp.int32)]
    position = jnp.concatenate([row_lengths[:staying], arrived_lengths])
    tokens_row = jnp.concatenate([row_tokens[:staying], arrived_tokens], axis=0)
    normed_attn = rms_scale(tokens_row.astype(jnp.float32), norm_first).astype(jnp.bfloat16)
    piece = lax.all_gather(project_in, "dp", axis=0, tiled=True)
    projected = jnp.dot(
        normed_attn,
        piece.reshape(piece.shape[0], 3 * head_cols),
        preferred_element_type=jnp.float32,
    )
    projected = projected.reshape(req_row, 3, heads_here, HD)
    query = rotate(projected[:, 0], position).astype(jnp.bfloat16)
    key_new = rotate(projected[:, 1], position).astype(jnp.bfloat16)
    value_new = projected[:, 2].astype(jnp.bfloat16)
    resident_cache = cache_pool[page_list[:staying]]
    cache_rows = jnp.concatenate([resident_cache, arrived_cache], axis=0).reshape(
        req_row, span_total, 2, heads_here, HD
    )
    key_rows = cache_rows[:, :, 0]
    value_rows = cache_rows[:, :, 1]
    scale_factor = HD ** (-0.5)
    scores = (
        jnp.einsum("nhd,nlhd->nhl", query, key_rows, preferred_element_type=jnp.float32)
        * scale_factor
    )
    valid_mask = jnp.arange(span_total, dtype=jnp.int32)[None, :] < position[:, None]
    scores = jnp.where(valid_mask[:, None, :], scores, -jnp.inf)
    own_score = (
        jnp.sum(query.astype(jnp.float32) * key_new.astype(jnp.float32), axis=-1) * scale_factor
    )
    highest = jnp.maximum(jnp.max(scores, axis=-1), own_score)
    weights_cache = jnp.exp(scores - highest[..., None])
    weight_own = jnp.exp(own_score - highest)
    denominator = jnp.sum(weights_cache, axis=-1) + weight_own
    probs_cache = (weights_cache / denominator[..., None]).astype(jnp.bfloat16)
    prob_own = (weight_own / denominator).astype(jnp.bfloat16)
    mixture = jnp.einsum(
        "nhl,nlhd->nhd", probs_cache, value_rows, preferred_element_type=jnp.float32
    )
    mixture = mixture + prob_own.astype(jnp.float32)[..., None] * value_new.astype(jnp.float32)
    heads_out = mixture.astype(jnp.bfloat16).reshape(req_row, head_cols)
    out_columns = lax.all_gather(project_out, "dp", axis=1, tiled=True)
    attn_proj = lax.psum_scatter(
        jnp.dot(heads_out, out_columns, preferred_element_type=jnp.float32),
        "fsdp",
        scatter_dimension=0,
        tiled=True,
    )
    mine_tokens = lax.dynamic_slice_in_dim(tokens_row, my_column * req_local, req_local, 0)
    resid = mine_tokens.astype(jnp.float32) + attn_proj
    moe_in = rms_scale(resid, norm_second).astype(jnp.bfloat16)
    logits = jnp.dot(moe_in, router, preferred_element_type=jnp.float32)
    expert_ids = jnp.arange(expert_count, dtype=jnp.int32)
    picked = routes[:, :, None] == expert_ids[None, None, :]
    chosen = jnp.sum(jnp.where(picked, logits[:, None, :], 0.0), axis=-1)
    weight_pair = jnp.stack(
        [jax.nn.sigmoid(chosen[:, 0] - chosen[:, 1]), jax.nn.sigmoid(chosen[:, 1] - chosen[:, 0])],
        axis=1,
    )
    mix_expert = jnp.sum(picked.astype(jnp.float32) * weight_pair[:, :, None], axis=1)
    member = jnp.sum(picked.astype(jnp.int32), axis=1)
    rank_expert = jnp.cumsum(member, axis=0) - member
    row_numbers = jnp.arange(rows_count, dtype=jnp.int32)
    expert_of_row = (row_numbers[:, None] // rows_per_expert == expert_ids[None, :]).astype(
        jnp.int32
    )
    replica_of_row = row_numbers % rows_per_expert
    member_row = jnp.sum(member[:, None, :] * expert_of_row[None, :, :], axis=-1)
    rank_row = jnp.sum(rank_expert[:, None, :] * expert_of_row[None, :, :], axis=-1)
    mix_row = jnp.sum(
        mix_expert[:, None, :] * expert_of_row[None, :, :].astype(jnp.float32), axis=-1
    )
    slot_ids = jnp.arange(slots_row, dtype=jnp.int32)
    wanted_rank = slot_ids[None, :, None] * rows_per_expert + replica_of_row[:, None, None]
    select = (member_row.T[:, None, :] == 1) & (rank_row.T[:, None, :] == wanted_rank)
    dispatch = jnp.einsum(
        "dst,tm->dsm", select.astype(jnp.bfloat16), moe_in, preferred_element_type=jnp.float32
    ).astype(jnp.bfloat16)
    received = lax.all_to_all(dispatch, "dp", split_axis=0, concat_axis=0, tiled=True)
    expert_tokens = lax.all_gather(received[None], "fsdp", axis=0, tiled=True)
    gate_whole, down_whole = (
        lax.all_to_all(gate_send, "dp", split_axis=0, concat_axis=1, tiled=True),
        lax.all_to_all(down_send, "dp", split_axis=0, concat_axis=1, tiled=True),
    )
    flattened = expert_tokens.reshape(-1, model_width)
    units_here = gate_up.shape[3]
    gate_cols = gate_whole[0].reshape(model_width, 2 * units_here)
    down_cols = down_whole[0]
    both_parts = jnp.dot(flattened, gate_cols, preferred_element_type=jnp.float32)
    activation = (jax.nn.silu(both_parts[:, :units_here]) * both_parts[:, units_here:]).astype(
        jnp.bfloat16
    )
    returned = lax.psum_scatter(
        lax.dot_general(
            activation, down_cols, (((1,), (1,)), ((), ())), preferred_element_type=jnp.float32
        ).astype(jnp.bfloat16),
        "fsdp",
        scatter_dimension=0,
        tiled=True,
    ).astype(jnp.float32)
    back_rows = lax.all_to_all(
        returned.reshape(rows_count, slots_row, model_width),
        "dp",
        split_axis=0,
        concat_axis=0,
        tiled=True,
    )
    coefficient = select.astype(jnp.float32) * mix_row.T[:, None, :]
    moe_total = jnp.einsum("dst,dsm->tm", coefficient, back_rows, precision=lax.Precision.HIGHEST)
    return (resid + moe_total).astype(jnp.bfloat16)


def solution(mesh):
    placed = (
        P(("dp", "fsdp"), None),
        P("dp", None, None, "fsdp"),
        P("dp", None, "fsdp"),
        P("fsdp", "dp"),
        P(),
        P(),
        P(),
        P(None, "dp", None, "fsdp"),
        P(None, "dp", "fsdp"),
        P(),
        P("dp", None),
        P("dp", None),
        P("dp"),
        P(),
        P(("dp", "fsdp"), None),
    )
    return jax.shard_map(
        local, mesh=mesh, in_specs=placed, out_specs=P(("dp", "fsdp"), None), check_vma=False
    )
```

profile of v0, /device:TPU:1, one launch (start us, length us, event | category | flops | bytes accessed | tf_op | source)
XLA Modules:
  0.0 533.4 jit_solution(7687817300184575141)
XLA Ops:
  7.3 20.2 %all_gather.12 = bf16[128,2304]{1,0:T(8,128)(2,1)S(1)} all-gather(bf16[8,2304]{1,0:T(8,128)(2,1)} %param.15), channel_id=1, replica_groups=mesh['dp'=16,'fsdp'=16] {'fsdp'}, dimensions={0}, use_global_device_ids=true | all-gather | bytes 626688 | tf_op jit(solution)/shard_map/all_gather | solution.py:71
  30.5 14.2 %all-to-all-start = ((bf16[16,2,1152]{2,1,0:T(2,128)(2,1)}), bf16[16,2,1152]{2,1,0:T(2,128)(2,1)S(1)}, u32[]{:S(2)}, u32[]{:S(2)}) async-start(bf16[16,2,1152]{2,1,0:T(2,128)(2,1)} %reshape.422), calls=%async_computation | async-start | bytes 147456 | tf_op jit(solution)/shard_map/all_to_all | solution.py:90
  47.0 3.8 gather_fusion.2
  51.5 1.9 copy.108
  53.7 27.4 %gather_fusion.1 = bf16[960,16,2,128]{3,2,1,0:T(2,128)(2,1)} fusion(bf16[528,16,2,128]{3,2,1,0:T(2,128)(2,1)} %param.16, s32[1024]{0:T(1024)S(1)} %pad_clamp_fusion.1), kind=kCustom, calls=%fused_computation.1 | custom fusion | bytes 15732480 | tf_op jit(solution)/shard_map/gather | solution.py:118
  81.0 7.4 %copy.105 = bf16[960,16,2,128]{3,1,2,0:T(8,128)(2,1)} copy(bf16[960,16,2,128]{3,2,1,0:T(2,128)(2,1)} %gather_fusion.1) | data formatting | bytes 15728640 | tf_op jit(solution)/shard_map/gather | solution.py:118
  88.4 7.4 %all-to-all-start.1 = ((bf16[16,8,16,2,128]{4,3,2,1,0:T(2,128)(2,1)}), bf16[16,8,16,2,128]{4,3,2,1,0:T(2,128)(2,1)S(1)}, u32[]{:S(2)}, u32[]{:S(2)}) async-start(bf16[16,8,16,2,128]{4,3,2,1,0:T(2,128)(2,1)} %copy.108), calls=%async_computation.1 | async-start | bytes 2097152 | tf_op jit(solution)/shard_map/all_to_all | solution.py:89
  97.1 37.6 %all_gather.14 = bf16[128,2304]{0,1:T(8,128)(2,1)S(1)} all-gather(bf16[128,144]{0,1:T(8,128)(2,1)S(1)} %copy-done.3), channel_id=1, replica_groups=mesh['dp'=16,'fsdp'=16] {'dp'}, dimensions={1}, use_global_device_ids=true | all-gather | bytes 626688 | tf_op jit(solution)/shard_map/all_gather | solution.py:145
  135.9 7.0 %pad_maximum_fusion = bf16[128,8,16,2,128]{4,2,3,1,0:T(8,128)(2,1)} fusion(bf16[8,8,16,2,128]{4,2,3,1,0:T(8,128)(2,1)S(1)} %copy.110, bf16[120,8,16,2,128]{4,2,3,1,0:T(8,128)(2,1)} %bitcast.84), kind=kLoop, calls=%fused_computation.3 | loop fusion | flops 4194304 | bytes 16777216 | tf_op jit(solution)/shard_map/concatenate | solution.py:119
  143.0 13.0 %copy.111 = bf16[128,8,16,2,128]{0,4,3,2,1:T(8,128)(2,1)} copy(bf16[128,8,16,2,128]{4,2,3,1,0:T(8,128)(2,1)} %pad_maximum_fusion) | data formatting | bytes 16777216 | tf_op jit(solution)/shard_map/concatenate | solution.py:119
  156.0 3.8 copy.103
  159.8 2.2 fusion.9
  162.0 3.9 multiply_reduce_fusion.1
  166.7 3.3 multiply_reduce_fusion
  170.1 1.4 fusion.53
  173.1 91.8 %all-reduce.3.cloned.1.call-done = f32[128,2304]{1,0:T(8,128)} async-done(((f32[128,2304]{1,0:T(8,128)}), f32[128,2304]{1,0:T(8,128)}) %all-reduce.3.cloned.1.call-update) | async-done | bytes 1179664
  264.9 1.0 multiply_reduce_fusion.2
  266.3 18.5 %all_to_all.45 = bf16[16,2,2304]{2,1,0:T(2,128)(2,1)} all-to-all(bf16[16,2,2304]{2,1,0:T(2,128)(2,1)S(1)} %copy.112), channel_id=1, replica_groups=mesh['dp'=16,'fsdp'=16] {'dp'}, dimensions={0} | all-to-all | bytes 294912 | tf_op jit(solution)/shard_map/all_to_all | solution.py:182
  284.7 5.1 broadcast_in_dim.37
  289.9 4.5 all-to-all-start.3
  295.1 78.4 %all-to-all-done.3 = bf16[16,144,2,360]{3,2,1,0:T(2,128)(2,1)} async-done(((bf16[16,144,2,360]{3,2,1,0:T(2,128)(2,1)}), bf16[16,144,2,360]{3,2,1,0:T(2,128)(2,1)}, u32[]{:S(2)}, u32[]{:S(2)}) %all-to-all-start.3) | async-done | bytes 3317792 | tf_op jit(solution)/shard_map/all_to_all | solution.py:185
  373.6 1.4 broadcast_in_dim.38
  375.0 5.5 %all-to-all-start.4 = ((bf16[16,144,360]{2,1,0:T(8,128)(2,1)}), bf16[16,144,360]{2,1,0:T(8,128)(2,1)}, u32[]{:S(2)}, u32[]{:S(2)}) async-start(bf16[16,144,360]{2,1,0:T(8,128)(2,1)} %bitcast.30), calls=%async_computation.4 | async-start | bytes 3538944 | tf_op jit(solution)/shard_map/all_to_all | solution.py:186
  380.7 8.5 %reshape_squeeze.3 = bf16[2304,720]{1,0:T(8,128)(2,1)} reshape(bf16[16,144,2,360]{3,2,1,0:T(2,128)(2,1)} %all-to-all-done.3) | data formatting | bytes 6635520 | tf_op jit(solution)/shard_map/reshape;squeeze | solution.py:190
  389.2 4.9 reshape.373
  394.2 5.1 fusion.54
  399.2 23.7 %all-to-all-done.4 = bf16[16,144,360]{2,1,0:T(8,128)(2,1)} async-done(((bf16[16,144,360]{2,1,0:T(8,128)(2,1)}), bf16[16,144,360]{2,1,0:T(8,128)(2,1)}, u32[]{:S(2)}, u32[]{:S(2)}) %all-to-all-start.4) | async-done | bytes 1658912 | tf_op jit(solution)/shard_map/all_to_all | solution.py:186
  422.9 4.9 convolution_convert_fusion
  428.2 74.2 %reduce-scatter.2.cloned.1.call-done = bf16[32,2304]{1,0:T(8,128)(2,1)} async-done(((bf16[512,2304]{1,0:T(8,128)(2,1)}), bf16[32,2304]{1,0:T(8,128)(2,1)}) %reduce-scatter.2.cloned.1.call-update) | async-done | bytes 147472 | tf_op jit(solution)/shard_map/reduce_scatter | solution.py:196
  502.4 1.8 reshape.380
  504.2 9.4 %all-to-all-start.5 = ((f32[16,2,2304]{2,1,0:T(2,128)}), f32[16,2,2304]{2,1,0:T(2,128)S(1)}, u32[]{:S(2)}, u32[]{:S(2)}) async-start(f32[16,2,2304]{2,1,0:T(2,128)} %reshape.380), calls=%async_computation.6 | async-start | bytes 589824 | tf_op jit(solution)/shard_map/all_to_all | solution.py:204
  513.7 12.2 %all-to-all-done.5 = f32[16,2,2304]{2,1,0:T(2,128)S(1)} async-done(((f32[16,2,2304]{2,1,0:T(2,128)}), f32[16,2,2304]{2,1,0:T(2,128)S(1)}, u32[]{:S(2)}, u32[]{:S(2)}) %all-to-all-start.5) | async-done | bytes 294944 | tf_op jit(solution)/shard_map/all_to_all | solution.py:204
  (98 shorter events, 13.8 us)
Async XLA Ops:
  6.5 421.3 %copy-start = (bf16[2304,8]{0,1:T(8,128)(2,1)S(1)}, bf16[2304,8]{0,1:T(8,128)(2,1)}, u32[]{:S(2)}) copy-start(bf16[2304,8]{0,1:T(8,128)(2,1)} %param.21) | copy-start | bytes 110596
  6.5 149.4 %all-gather.4.cloned.1.call-start = ((), (), s32[]{:S(2)}) async-start(), calls=%async_computation.7 | async-start | bytes 1880064 | tf_op jit(solution)/shard_map/all_gather | solution.py:108
  30.5 58.0 %all-to-all-start = ((bf16[16,2,1152]{2,1,0:T(2,128)(2,1)}), bf16[16,2,1152]{2,1,0:T(2,128)(2,1)S(1)}, u32[]{:S(2)}, u32[]{:S(2)}) async-start(bf16[16,2,1152]{2,1,0:T(2,128)(2,1)} %reshape.422), calls=%async_computation | async-start | bytes 147456 | tf_op jit(solution)/shard_map/all_to_all | solution.py:90
  81.0 7.4 %copy-start.6 = (bf16[2304]{0:T(1024)(128)(2,1)S(1)}, bf16[2304]{0:T(1024)(128)(2,1)}, u32[]{:S(2)}) copy-start(bf16[2304]{0:T(1024)(128)(2,1)} %param.19) | copy-start | bytes 13828
  81.0 14.8 %copy-start.4 = (s32[16,8]{0,1:T(8,128)S(1)}, s32[16,8]{0,1:T(8,128)}, u32[]{:S(2)}) copy-start(s32[16,8]{0,1:T(8,128)} %param.28) | copy-start | bytes 1540
  88.4 7.6 %copy-start.1 = (s32[2048]{0:T(1024)S(1)}, s32[2048]{0:T(1024)}, u32[]{:S(2)}) copy-start(s32[2048]{0:T(1024)} %param.24) | copy-start | bytes 24580
  88.4 8.6 %copy-start.3 = (bf16[128,144]{0,1:T(8,128)(2,1)S(1)}, bf16[128,144]{0,1:T(8,128)(2,1)}, u32[]{:S(2)}) copy-start(bf16[128,144]{0,1:T(8,128)(2,1)} %param.18) | copy-start | bytes 110596
  88.4 46.7 %all-to-all-start.1 = ((bf16[16,8,16,2,128]{4,3,2,1,0:T(2,128)(2,1)}), bf16[16,8,16,2,128]{4,3,2,1,0:T(2,128)(2,1)S(1)}, u32[]{:S(2)}, u32[]{:S(2)}) async-start(bf16[16,8,16,2,128]{4,3,2,1,0:T(2,128)(2,1)} %copy.108), calls=%async_computation.1 | async-start | bytes 2097152 | tf_op jit(solution)/shard_map/all_to_all | solution.py:89
  95.8 169.1 %all-reduce.3.cloned.1.call-start = ((), (), s32[]{:S(2)}) async-start(), calls=%async_computation.10 | async-start | bytes 2359296
  170.0 1.5 copy-start.5
  170.0 1.6 copy-start.7
  170.0 1.6 copy-start.8
  289.9 83.7 %copy-start.2 = (bf16[8,144,360]{2,1,0:T(8,128)(2,1)S(1)}, bf16[8,144,360]{2,1,0:T(8,128)(2,1)}, u32[]{:S(2)}) copy-start(bf16[8,144,360]{2,1,0:T(8,128)(2,1)} %param.23) | copy-start | bytes 2488324
  289.9 83.7 %all-to-all-start.3 = ((bf16[16,144,2,360]{3,2,1,0:T(2,128)(2,1)}), bf16[16,144,2,360]{3,2,1,0:T(2,128)(2,1)}, u32[]{:S(2)}, u32[]{:S(2)}) async-start(bf16[16,144,2,360]{3,2,1,0:T(2,128)(2,1)} %bitcast.85), calls=%async_computation.3 | async-start | bytes 7077888 | tf_op jit(solution)/shard_map/all_to_all | solution.py:185
  294.4 94.8 %all-gather.6.cloned.1.call-start = ((), (), s32[]{:S(2)}) async-start(), calls=%async_computation.9 | async-start | bytes 2506752 | tf_op jit(solution)/shard_map/all_gather | solution.py:183
  375.0 48.0 %all-to-all-start.4 = ((bf16[16,144,360]{2,1,0:T(8,128)(2,1)}), bf16[16,144,360]{2,1,0:T(8,128)(2,1)}, u32[]{:S(2)}, u32[]{:S(2)}) async-start(bf16[16,144,360]{2,1,0:T(8,128)(2,1)} %bitcast.30), calls=%async_computation.4 | async-start | bytes 3538944 | tf_op jit(solution)/shard_map/all_to_all | solution.py:186
  380.4 122.0 %reduce-scatter.2.cloned.1.call-start = ((), (), s32[]{:S(2)}) async-start(), calls=%async_computation.8 | async-start | bytes 2506752 | tf_op jit(solution)/shard_map/reduce_scatter | solution.py:196
  504.2 21.7 %all-to-all-start.5 = ((f32[16,2,2304]{2,1,0:T(2,128)}), f32[16,2,2304]{2,1,0:T(2,128)S(1)}, u32[]{:S(2)}, u32[]{:S(2)}) async-start(f32[16,2,2304]{2,1,0:T(2,128)} %reshape.380), calls=%async_computation.6 | async-start | bytes 589824 | tf_op jit(solution)/shard_map/all_to_all | solution.py:204
Sparse Core Ops, SparseCore 0:
  9.2 43.5 all-gather.3
  171.6 93.2 all-reduce.2
  297.7 48.1 all-gather.5
  427.9 74.4 reduce-scatter.1
where the time goes:
time: 535 us; the launch traced here: 533 us
  waiting for transfers between devices  282 us (53%)
  local copies, waits for them, and re-layouts  83.3 us (16%)
  blocking collectives  76.3 us (14%)
  starting transfers between devices  41.3 us (8%)
  other arithmetic  20 us (4%)
  matrix products  16.5 us (3%)
  between operations  14.2 us (3%)
    unnamed x5, waiting for transfers between devices  93.2 us
    all_to_all x1, waiting for transfers between devices, local(): lax.all_to_all(gate_send, 'dp', split_axis=0, concat_axis=1, tiled=True)  78.4 us
    reduce_scatter x1, waiting for transfers between devices, local(): lax.psum_scatter(lax.dot_general(activation, down_cols, (((1,), (1,)), ((...  74.2 us
    all_gather x1, blocking collectives, local(): out_columns = lax.all_gather(project_out, 'dp', axis=1, tiled=True)  37.6 us
    gather x2, local copies, waits for them, and re-layouts, local(): resident_cache = cache_pool[page_list[:staying]]  34.7 us
    all_to_all x1, waiting for transfers between devices, local(): lax.all_to_all(down_send, 'dp', split_axis=0, concat_axis=1, tiled=True)  23.7 us
    all_gather x1, blocking collectives, local(): row_tokens = lax.all_gather(hidden_in, 'fsdp', axis=0, tiled=True)  20.2 us
    all_to_all x1, blocking collectives, local(): lax.all_to_all(dispatch, 'dp', split_axis=0, concat_axis=0, tiled=True)  18.5 us
  transfers between devices with their start and end apart: 9, of which 5 were waited for; matrix products, arithmetic and copies ran while one was open for 17% of the time, Pallas kernels for 0%

commit v1 on v0

v1 whole, which is shorter than its diff:
```python
import functools

import jax
import jax.numpy as jnp
from jax import lax
from jax.experimental import pallas as pl
from jax.experimental.pallas import tpu as pltpu
from jax.sharding import PartitionSpec as P

HD = 64
CAP = 4
LOW = -1e30
F32 = jnp.float32
BF16 = jnp.bfloat16


def vmem():
    return pl.BlockSpec(memory_space=pltpu.VMEM)


def rms_scale(values, scaling):
    return (
        values
        * lax.rsqrt(jnp.mean(values * values, axis=-1, keepdims=True) + 1e-06)
        * scaling.astype(F32)
    )


def dot_t(left, right):
    return lax.dot_general(left, right, (((1,), (1,)), ((), ())), preferred_element_type=F32)


def attention_kernel(
    page_len, tokens_ref, norm_ref, weight_ref, cos_ref, sin_ref, limit_ref, cache_ref, out_ref, wide_ref, score_ref
):
    pages = limit_ref.shape[1]
    count, width = out_ref.shape
    heads = width // HD
    wide_ref[...] = cache_ref[...].astype(F32)
    normed = rms_scale(tokens_ref[...].astype(F32), norm_ref[...]).astype(BF16)
    parts = [jnp.dot(normed, weight_ref[i], preferred_element_type=F32) for i in range(3)]
    lane = lax.broadcasted_iota(jnp.int32, (count, width), 1)
    low_half = lane % HD < HD // 2

    def rotate(values):
        partner = jnp.where(
            low_half,
            pltpu.roll(values, width - HD // 2, 1),
            pltpu.roll(values, HD // 2, 1),
        )
        return (values * cos_ref[...] + partner * sin_ref[...]).astype(BF16)

    query = rotate(parts[0])
    key_new = rotate(parts[1])
    value_new = parts[2].astype(BF16)
    head_lane = lax.broadcasted_iota(jnp.int32, (heads, count, width), 2) // HD
    head_row = lax.broadcasted_iota(jnp.int32, (heads, count, width), 0)
    wide_query = query.astype(F32)
    spread = jnp.where(head_lane == head_row, wide_query[None], 0.0)
    scale = HD ** (-0.5)
    own_score = jnp.sum(spread * key_new.astype(F32)[None], axis=-1, keepdims=True) * scale
    spread_query = spread.reshape(heads * count, width).astype(BF16)
    own_score = own_score.reshape(heads * count, 1)

    def score_step(u, highest):
        keys = wide_ref[pl.ds(2 * u, pages, stride=2 * page_len), :].astype(BF16)
        scores = dot_t(spread_query, keys) * scale
        scores = jnp.where((limit_ref[...] > u)[None], scores.reshape(heads, count, pages), LOW)
        scores = scores.reshape(heads * count, pages)
        score_ref[u] = scores
        return jnp.maximum(highest, scores)

    highest = lax.fori_loop(
        0, page_len, score_step, jnp.full((heads * count, pages), LOW, F32)
    )
    highest = jnp.maximum(jnp.max(highest, axis=-1, keepdims=True), own_score)

    def value_step(u, carry):
        total, mixture = carry
        weights = jnp.exp(score_ref[u] - highest)
        values = wide_ref[pl.ds(2 * u + 1, pages, stride=2 * page_len), :].astype(BF16)
        mixture = mixture + jnp.dot(weights.astype(BF16), values, preferred_element_type=F32)
        return total + jnp.sum(weights, axis=-1, keepdims=True), mixture

    weight_own = jnp.exp(own_score - highest)
    total, mixture = lax.fori_loop(
        0,
        page_len,
        value_step,
        (weight_own, jnp.zeros((heads * count, width), F32)),
    )
    mixture = (mixture / total).reshape(heads, count, width)
    prob_own = (weight_own / total).astype(BF16).astype(F32).reshape(heads, count, 1)
    mixture = mixture + prob_own * value_new.astype(F32)[None]
    out_ref[...] = jnp.sum(jnp.where(head_lane == head_row, mixture, 0.0), axis=0).astype(BF16)


def attention(tokens, norm, weight, position, limit, cache_pool):
    count = tokens.shape[0]
    pages, page_len, _, width = cache_pool.shape
    channel = (jnp.arange(width, dtype=jnp.int32) % (HD // 2)).astype(F32)
    inverse = jnp.exp(-jnp.log(10000.0) * 2.0 * channel / HD)
    angles = position.astype(F32)[:, None] * inverse
    sign = jnp.where(jnp.arange(width) % HD < HD // 2, -1.0, 1.0)
    rows = pages * page_len * 2
    return pl.pallas_call(
        functools.partial(attention_kernel, page_len),
        out_shape=jax.ShapeDtypeStruct((count, width), BF16),
        in_specs=[vmem()] * 7,
        out_specs=vmem(),
        scratch_shapes=[
            pltpu.VMEM((rows, width), F32),
            pltpu.VMEM((page_len, count * (width // HD), pages), F32),
        ],
        compiler_params=pltpu.CompilerParams(vmem_limit_bytes=56 * 1024 * 1024),
        name="attention",
    )(
        tokens,
        norm[None, :],
        weight,
        jnp.cos(angles),
        jnp.sin(angles) * sign,
        limit,
        cache_pool.reshape(rows, width),
    )


def local(
    hidden_in,
    cache_pool,
    project_in,
    project_out,
    norm_first,
    norm_second,
    router,
    gate_up,
    expert_down,
    lengths,
    prompt_pages,
    own_pages,
    groups,
    move_target,
    routes,
):
    rows_count = lax.axis_size("dp")
    fsdp_count = lax.axis_size("fsdp")
    my_row = lax.axis_index("dp")
    my_column = lax.axis_index("fsdp")
    req_local, model_width = hidden_in.shape
    req_row = req_local * fsdp_count
    movers = move_target.shape[1]
    staying = req_row - movers
    pages, page_len = cache_pool.shape[:2]
    head_cols = cache_pool.shape[3]
    expert_count = router.shape[1]
    rows_per_expert = rows_count // expert_count
    slots_row = (CAP + rows_per_expert - 1) // rows_per_expert
    units_here = gate_up.shape[3]
    features_here = gate_up.shape[1]

    same_core = [list(range(k, rows_count, rows_per_expert)) for k in range(rows_per_expert)]

    def spread_weights(values):
        return lax.all_to_all(
            values, "dp", split_axis=0, concat_axis=0, tiled=True, axis_index_groups=same_core
        )

    gate_half = spread_weights(jnp.transpose(gate_up, (0, 2, 1, 3)))
    down_half = spread_weights(expert_down)

    row_tokens = lax.all_gather(hidden_in, "fsdp", axis=0, tiled=True)
    weight_in = lax.all_gather(jnp.transpose(project_in, (1, 0, 2)), "dp", axis=1, tiled=True)
    weight_out = lax.all_gather(project_out.T, "dp", axis=0, tiled=True)
    group_hit = (
        groups[:, None] == jnp.arange(prompt_pages.shape[0], dtype=jnp.int32)[None, :]
    ).astype(jnp.int32)
    prompt_list = jnp.sum(group_hit[:, :, None] * prompt_pages[None, :, :], axis=1)
    page_list = jnp.concatenate([prompt_list, own_pages], axis=1)
    position = lax.dynamic_slice_in_dim(lengths, my_row * req_row, req_row)
    page_numbers = jnp.arange(pages, dtype=jnp.int32)
    limit = jnp.zeros((req_row, pages), jnp.int32)
    for j in range(page_list.shape[1]):
        valid = jnp.clip(position - page_len * j, 0, page_len)
        limit += jnp.where(page_list[:, j : j + 1] == page_numbers[None, :], valid[:, None], 0)

    heads_out = attention(row_tokens, norm_first, weight_in, position, limit, cache_pool)

    row_numbers = jnp.arange(rows_count, dtype=jnp.int32)
    send_select = (move_target[my_row][None, :] == row_numbers[:, None]).astype(BF16)
    leaving = jnp.concatenate([heads_out[staying:], row_tokens[staying:]], axis=1)
    leaving_send = jnp.dot(send_select, leaving, preferred_element_type=F32).astype(BF16)
    leaving_recv = lax.all_to_all(leaving_send, "dp", split_axis=0, concat_axis=0, tiled=True)
    arrive_select = (move_target == my_row).astype(BF16)
    arrived = lax.dot_general(
        arrive_select, leaving_recv, (((0,), (0,)), ((), ())), preferred_element_type=F32
    ).astype(BF16)
    heads_row = jnp.concatenate([heads_out[:staying], arrived[:, :head_cols]], axis=0)
    mine_tokens = jnp.where(
        my_column == fsdp_count - 1, arrived[:, head_cols:], hidden_in
    )
    partial_out = dot_t(heads_row, weight_out).astype(BF16)
    partial_recv = lax.all_to_all(
        partial_out.reshape(fsdp_count, req_local, model_width),
        "fsdp",
        split_axis=0,
        concat_axis=0,
        tiled=True,
    )
    attn_proj = jnp.sum(partial_recv.astype(F32), axis=0)
    resid = mine_tokens.astype(F32) + attn_proj
    moe_in = rms_scale(resid, norm_second).astype(BF16)
    logits = jnp.dot(moe_in, router, preferred_element_type=F32)
    expert_ids = jnp.arange(expert_count, dtype=jnp.int32)
    picked = routes[:, :, None] == expert_ids[None, None, :]
    chosen = jnp.sum(jnp.where(picked, logits[:, None, :], 0.0), axis=-1)
    weight_pair = jnp.stack(
        [jax.nn.sigmoid(chosen[:, 0] - chosen[:, 1]), jax.nn.sigmoid(chosen[:, 1] - chosen[:, 0])],
        axis=1,
    )
    mix_expert = jnp.sum(picked.astype(F32) * weight_pair[:, :, None], axis=1)
    member = jnp.sum(picked.astype(jnp.int32), axis=1)
    rank_expert = jnp.cumsum(member, axis=0) - member
    expert_of_row = (row_numbers[:, None] // rows_per_expert == expert_ids[None, :]).astype(
        jnp.int32
    )
    replica_of_row = row_numbers % rows_per_expert
    member_row = jnp.sum(member[:, None, :] * expert_of_row[None, :, :], axis=-1)
    rank_row = jnp.sum(rank_expert[:, None, :] * expert_of_row[None, :, :], axis=-1)
    mix_row = jnp.sum(mix_expert[:, None, :] * expert_of_row[None, :, :].astype(F32), axis=-1)
    slot_ids = jnp.arange(slots_row, dtype=jnp.int32)
    wanted_rank = slot_ids[None, :, None] * rows_per_expert + replica_of_row[:, None, None]
    select = (member_row.T[:, None, :] == 1) & (rank_row.T[:, None, :] == wanted_rank)
    dispatch = jnp.einsum(
        "dst,tm->dsm", select.astype(BF16), moe_in, preferred_element_type=F32
    ).astype(BF16)
    received = lax.all_to_all(dispatch, "dp", split_axis=0, concat_axis=0, tiled=True)
    expert_tokens = lax.all_gather(received[None], "fsdp", axis=0, tiled=True)
    flattened = expert_tokens.reshape(-1, model_width)

    swap = [(d, d ^ 1) for d in range(rows_count)]
    first_core = my_row % 2 == 0

    def both(values):
        other = lax.ppermute(values, "dp", swap)
        return jnp.stack(
            [jnp.where(first_core, values, other), jnp.where(first_core, other, values)], axis=1
        )

    gate_whole = both(gate_half)
    down_whole = both(down_half)
    down_cols = down_whole.reshape(model_width, units_here)
    gate_cols = gate_whole[:, :, 0].reshape(model_width, units_here)
    up_cols = gate_whole[:, :, 1].reshape(model_width, units_here)
    gate_part = jnp.dot(flattened, gate_cols, preferred_element_type=F32)
    up_part = jnp.dot(flattened, up_cols, preferred_element_type=F32)
    activation = (jax.nn.silu(gate_part) * up_part).astype(BF16)
    expert_y = dot_t(activation, down_cols).astype(BF16)
    returned = lax.all_to_all(
        expert_y.reshape(fsdp_count, rows_count * slots_row, model_width),
        "fsdp",
        split_axis=0,
        concat_axis=0,
        tiled=True,
    )
    returned = jnp.sum(returned.astype(F32), axis=0).astype(BF16)
    back_rows = lax.all_to_all(
        returned.reshape(rows_count, slots_row, model_width),
        "dp",
        split_axis=0,
        concat_axis=0,
        tiled=True,
    )
    coefficient = select.astype(F32) * mix_row.T[:, None, :]
    moe_total = jnp.einsum(
        "dst,dsm->tm", coefficient, back_rows.astype(F32), precision=lax.Precision.HIGHEST
    )
    return (resid + moe_total).astype(BF16)


def solution(mesh):
    placed = (
        P(("dp", "fsdp"), None),
        P("dp", None, None, "fsdp"),
        P("dp", None, "fsdp"),
        P("fsdp", "dp"),
        P(),
        P(),
        P(),
        P(None, "dp", None, "fsdp"),
        P(None, "dp", "fsdp"),
        P(),
        P("dp", None),
        P("dp", None),
        P("dp"),
        P(),
        P(("dp", "fsdp"), None),
    )
    return jax.shard_map(
        local, mesh=mesh, in_specs=placed, out_specs=P(("dp", "fsdp"), None), check_vma=False
    )
```

time: 535 us -> 313 us (0.59)
  waiting for transfers between devices: 282 us -> 92.3 us
  local copies, waits for them, and re-layouts: 83.3 us -> 13.3 us
  blocking collectives: 76.3 us -> 103 us
  Pallas kernels: 0 us -> 22.6 us
  starting transfers between devices: 41.3 us -> 34.9 us
    unnamed x5 -> x2, waiting for transfers between devices: 93.2 us -> 0.7 us
    reduce_scatter x1 -> x0, waiting for transfers between devices: 74.2 us -> none  [local(): lax.psum_scatter(lax.dot_general(activation, down_cols, (((1,), (1,)), ((...]
    all_to_all x4, waiting for transfers between devices: 102 us -> 41.6 us  [the longest x1 30.8 us: local(): lax.all_to_all(expert_y.reshape(fsdp_count, rows_count * slots_row, model...]
    gather x4 -> x0, local copies, waits for them, and re-layouts: 39.2 us -> none  [the longest x2 34.7 us: local(): resident_cache = cache_pool[page_list[:staying]]]
    all_gather x1, waiting for transfers between devices: 0.01 us -> 25 us  [local(): expert_tokens = lax.all_gather(received[None], 'fsdp', axis=0, tiled=True)]
    pallas_call x0 -> x1, Pallas kernels: none -> 22.6 us  [attention(): pl.pallas_call(functools.partial(attention_kernel, page_len), out_shape=j...]
    all_gather x1, waiting for transfers between devices: 0.01 us -> 15.8 us  [local(): lax.all_gather(jnp.transpose(project_in, (1, 0, 2)), 'dp', axis=1, tiled=...]
    all_gather x1, blocking collectives: 37.6 us -> 52.9 us  [local(): weight_out = lax.all_gather(project_out.T, 'dp', axis=0, tiled=True)]
  transfers between devices with their start and end apart: 9 -> 9, of which waited for: 5 -> 5; matrix products, arithmetic and copies ran while one was open for 17% -> 10% of each run, Pallas kernels for 0% -> 7%
where the time goes in v1:
time: 313 us; the launch traced here: 312 us
  blocking collectives  103 us (33%)
  waiting for transfers between devices  92.3 us (29%)
  starting transfers between devices  34.9 us (11%)
  Pallas kernels  22.6 us (7%)
  other arithmetic  19.5 us (6%)
  between operations  13.7 us (4%)
  local copies, waits for them, and re-layouts  13.3 us (4%)
  matrix products  12.8 us (4%)
    all_gather x1, blocking collectives, local(): weight_out = lax.all_gather(project_out.T, 'dp', axis=0, tiled=True)  52.9 us
    all_to_all x1, waiting for transfers between devices, local(): lax.all_to_all(expert_y.reshape(fsdp_count, rows_count * slots_row, model...  30.8 us
    all_gather x1, waiting for transfers between devices, local(): expert_tokens = lax.all_gather(received[None], 'fsdp', axis=0, tiled=True)  25 us
    pallas_call x1, Pallas kernels, attention(): pl.pallas_call(functools.partial(attention_kernel, page_len), out_shape=j...  22.6 us
    all_gather x1, blocking collectives, local(): row_tokens = lax.all_gather(hidden_in, 'fsdp', axis=0, tiled=True)  21 us
    all_to_all x1, blocking collectives, local(): lax.all_to_all(dispatch, 'dp', split_axis=0, concat_axis=0, tiled=True)  16.1 us
    all_gather x1, waiting for transfers between devices, local(): lax.all_gather(jnp.transpose(project_in, (1, 0, 2)), 'dp', axis=1, tiled=...  15.8 us
    all_to_all x1, blocking collectives, local(): lax.all_to_all(leaving_send, 'dp', split_axis=0, concat_axis=0, tiled=True)  13.4 us
  transfers between devices with their start and end apart: 9, of which 5 were waited for; matrix products, arithmetic and copies ran while one was open for 10% of the time, Pallas kernels for 7%

profile of v1, /device:TPU:1, one launch (start us, length us, event | category | flops | bytes accessed | tf_op | source)
XLA Modules:
  0.0 312.4 jit_solution(14388369472216230434)
XLA Ops:
  7.3 9.0 %all-to-all-start.4 = ((bf16[8,144,360]{2,1,0:T(8,128)(2,1)}), bf16[8,144,360]{2,1,0:T(8,128)(2,1)S(1)}, u32[]{:S(2)}, u32[]{:S(2)}) async-start(bf16[8,144,360]{2,1,0:T(8,128)(2,1)} %param.23), calls=%async_computation.4 | async-start | bytes 1769472 | tf_op jit(solution)/shard_map/all_to_all | solution.py:164
  16.9 21.0 %all_gather.12.tokens_ref = bf16[128,2304]{1,0:T(8,128)(2,1)S(1)} all-gather(bf16[8,2304]{1,0:T(8,128)(2,1)S(1)} %copy-done.2), channel_id=1, replica_groups=mesh['dp'=16,'fsdp'=16] {'fsdp'}, dimensions={0}, use_global_device_ids=true | all-gather | bytes 626688 | tf_op jit(solution)/shard_map/all_gather | solution.py:171
  38.1 0.8 broadcast_clamp_fusion
  39.0 1.0 fusion.16
  40.0 1.1 select_add_fusion.limit_ref
  41.1 15.8 %all-gather.4.cloned.1.call-done.weight_ref = bf16[3,2304,128]{2,1,0:T(8,128)(2,1)} async-done(((bf16[3,144,128]{2,1,0:T(8,128)(2,1)}), bf16[3,2304,128]{2,1,0:T(8,128)(2,1)}) %all-gather.4.cloned.1.call-update) | async-done | bytes 1769488 | tf_op jit(solution)/shard_map/all_gather | solution.py:172
  56.8 22.6 %attention.1 = bf16[128,128]{1,0:T(8,128)(2,1)} custom-call(bf16[128,2304]{1,0:T(8,128)(2,1)} %copy-done.1, bf16[1,2304]{1,0:T(2,128)(2,1)} %broadcast_in_dim.123.norm_ref, bf16[3,2304,128]{2,1,0:T(8,128)(2,1)} %all-gather.4.cloned.1.call-done.weight_ref, f32[128,128]{1,0:T(8,128)} %get-tuple-element.28.cos_ref, f32[128,128]{1,0:T(8,128)} %get-tuple-element.27.sin_ref, ...), custom_call_target="tpu_custom_call" | custom-call | tf_op jit(solution)/shard_map/attention/pallas_call | solution.py:106
  80.9 0.7 reduce.3
  81.7 13.4 %all_to_all.42 = bf16[16,2,1216]{2,1,0:T(2,128)(2,1)S(1)} all-to-all(bf16[16,2,1216]{2,1,0:T(2,128)(2,1)S(1)} %reshape.235), channel_id=1, replica_groups=mesh['dp'=16,'fsdp'=16] {'dp'}, dimensions={0} | all-to-all | bytes 155648 | tf_op jit(solution)/shard_map/all_to_all | solution.py:192
  95.1 3.7 %all-to-all-start.3 = ((bf16[8,2,144,360]{3,1,2,0:T(2,128)(2,1)}), bf16[8,2,144,360]{3,1,2,0:T(2,128)(2,1)S(1)}, u32[]{:S(2)}, u32[]{:S(2)}) async-start(bf16[8,2,144,360]{3,1,2,0:T(2,128)(2,1)} %bitcast.61), calls=%async_computation.3 | async-start | bytes 3538944 | tf_op jit(solution)/shard_map/all_to_all | solution.py:164
  100.7 52.9 %all_gather.14 = bf16[2304,128]{1,0:T(8,128)(2,1)S(1)} all-gather(bf16[144,128]{1,0:T(8,128)(2,1)S(1)} %bitcast.66), channel_id=1, replica_groups=mesh['dp'=16,'fsdp'=16] {'dp'}, dimensions={0}, use_global_device_ids=true | all-gather | bytes 626688 | tf_op jit(solution)/shard_map/all_gather | solution.py:173
  154.5 0.8 convolution_convert_fusion.4
  155.3 1.9 fusion
  157.2 6.1 %all-to-all-start.1 = ((bf16[16,8,2304]{2,1,0:T(8,128)(2,1)}), bf16[16,8,2304]{2,1,0:T(8,128)(2,1)S(1)}, u32[]{:S(2)}, u32[]{:S(2)}) async-start(bf16[16,8,2304]{2,1,0:T(8,128)(2,1)} %fusion), calls=%async_computation.1 | async-start | bytes 1179648 | tf_op jit(solution)/shard_map/all_to_all | solution.py:202
  164.1 10.8 %all-to-all-done.1 = bf16[16,8,2304]{2,1,0:T(8,128)(2,1)S(1)} async-done(((bf16[16,8,2304]{2,1,0:T(8,128)(2,1)}), bf16[16,8,2304]{2,1,0:T(8,128)(2,1)S(1)}, u32[]{:S(2)}, u32[]{:S(2)}) %all-to-all-start.1) | async-done | bytes 589856 | tf_op jit(solution)/shard_map/all_to_all | solution.py:202
  175.5 16.1 %all_to_all.43 = bf16[16,2,2304]{2,1,0:T(2,128)(2,1)} all-to-all(bf16[16,2,2304]{2,1,0:T(2,128)(2,1)S(1)} %copy.48), channel_id=1, replica_groups=mesh['dp'=16,'fsdp'=16] {'dp'}, dimensions={0} | all-to-all | bytes 294912 | tf_op jit(solution)/shard_map/all_to_all | solution.py:236
  191.6 1.4 select_bitcast_fusion.1
  193.4 1.4 copy.51
  194.8 4.9 %fusion.4 = (bf16[8,1,2,144,360]{4,2,3,0,1:T(2,128)(2,1)S(1)}, bf16[8,1,2,144,360]{4,2,3,0,1:T(2,128)(2,1)S(1)}) fusion(bf16[8,2,144,360]{3,1,2,0:T(2,128)(2,1)S(1)} %all-to-all-done.3, bf16[8,2,144,360]{3,1,2,0:T(2,128)(2,1)} %collective-permute-done, pred[]{:T(512)S(6)} %eq.293), kind=kLoop, calls=%fused_computation.14 | loop fusion | flops 1658880 | bytes 6635521 | tf_op jit(solution)/shard_map/stack | solution.py:245
  199.7 6.4 %slice_maximum_fusion = (bf16[8,2,1,144,360]{4,2,3,0,1:T(2,128)(2,1)S(1)}, bf16[8,2,1,144,360]{4,2,3,0,1:T(2,128)(2,1)S(1)}) fusion(bf16[8,1,2,144,360]{4,2,3,0,1:T(2,128)(2,1)S(1)} %get-tuple-element.14, bf16[8,1,2,144,360]{4,2,3,0,1:T(2,128)(2,1)S(1)} %get-tuple-element.13), kind=kLoop, calls=%fused_computation.3 | loop fusion | flops 6635520 | bytes 6635520 | tf_op jit(solution)/shard_map/stack | solution.py:245
  206.1 1.6 copy.49
  207.6 1.5 copy.50
  209.1 25.0 %all-gather.6.cloned.1.call-done = bf16[256,2,2304]{2,1,0:T(2,128)(2,1)} async-done(((bf16[16,2,2304]{2,1,0:T(2,128)(2,1)}), bf16[256,2,2304]{2,1,0:T(2,128)(2,1)}) %all-gather.6.cloned.1.call-update) | async-done | bytes 2359312 | tf_op jit(solution)/shard_map/all_gather | solution.py:237
  234.2 4.9 %reshape.226 = bf16[512,2304]{1,0:T(8,128)(2,1)S(1)} reshape(bf16[256,2,2304]{2,1,0:T(2,128)(2,1)} %all-gather.6.cloned.1.call-done) | data formatting | bytes 4718592 | tf_op jit(solution)/shard_map/reshape | solution.py:238
  239.1 2.6 fusion.47
  241.7 6.0 %convolution_convert_fusion = bf16[512,2304]{1,0:T(8,128)(2,1)} fusion(bf16[2304,360]{1,0:T(8,128)(2,1)} %bitcast.62, bf16[512,2304]{1,0:T(8,128)(2,1)S(1)} %reshape.226, bf16[2304,360]{1,0:T(8,128)(2,1)} %bitcast.64, f32[512,360]{0,1:T(8,128)S(1)} %fusion.47), kind=kOutput, calls=%fused_computation | convolution fusion | flops 1700978688 | bytes 8773632 | tf_op jit(solution)/shard_map/dot_general | solution.py:30
  247.7 4.6 %all-to-all-start.5 = ((bf16[16,32,2304]{2,1,0:T(8,128)(2,1)}), bf16[16,32,2304]{2,1,0:T(8,128)(2,1)S(1)}, u32[]{:S(2)}, u32[]{:S(2)}) async-start(bf16[16,32,2304]{2,1,0:T(8,128)(2,1)} %bitcast.60), calls=%async_computation.5 | async-start | bytes 4718592 | tf_op jit(solution)/shard_map/all_to_all | solution.py:258
  252.8 30.8 %all-to-all-done.5 = bf16[16,32,2304]{2,1,0:T(8,128)(2,1)S(1)} async-done(((bf16[16,32,2304]{2,1,0:T(8,128)(2,1)}), bf16[16,32,2304]{2,1,0:T(8,128)(2,1)S(1)}, u32[]{:S(2)}, u32[]{:S(2)}) %all-to-all-start.5) | async-done | bytes 2359328 | tf_op jit(solution)/shard_map/all_to_all | solution.py:258
  283.9 0.7 reshape.229
  284.7 10.7 %all-to-all-start.6 = ((bf16[16,2,2304]{2,1,0:T(2,128)(2,1)}), bf16[16,2,2304]{2,1,0:T(2,128)(2,1)S(1)}, u32[]{:S(2)}, u32[]{:S(2)}) async-start(bf16[16,2,2304]{2,1,0:T(2,128)(2,1)} %reshape.229), calls=%async_computation.6 | async-start | bytes 294912 | tf_op jit(solution)/shard_map/all_to_all | solution.py:266
  295.5 9.1 %all-to-all-done.6 = bf16[16,2,2304]{2,1,0:T(2,128)(2,1)S(1)} async-done(((bf16[16,2,2304]{2,1,0:T(2,128)(2,1)}), bf16[16,2,2304]{2,1,0:T(2,128)(2,1)S(1)}, u32[]{:S(2)}, u32[]{:S(2)}) %all-to-all-start.6) | async-done | bytes 147488 | tf_op jit(solution)/shard_map/all_to_all | solution.py:266
  304.7 0.9 fusion.3
  (83 shorter events, 8.5 us)
Async XLA Ops:
  6.5 245.8 %copy-start = (bf16[2304,8]{0,1:T(8,128)(2,1)S(1)}, bf16[2304,8]{0,1:T(8,128)(2,1)}, u32[]{:S(2)}) copy-start(bf16[2304,8]{0,1:T(8,128)(2,1)} %param.21) | copy-start | bytes 110596
  6.5 9.8 %copy-start.11 = (bf16[2304]{0:T(1024)(128)(2,1)S(1)}, bf16[2304]{0:T(1024)(128)(2,1)}, u32[]{:S(2)}) copy-start(bf16[2304]{0:T(1024)(128)(2,1)} %param.19) | copy-start | bytes 13828
  6.5 10.4 %copy-start.2 = (bf16[8,2304]{1,0:T(8,128)(2,1)S(1)}, bf16[8,2304]{1,0:T(8,128)(2,1)}, u32[]{:S(2)}) copy-start(bf16[8,2304]{1,0:T(8,128)(2,1)} %param.15) | copy-start | bytes 110596
  6.5 31.4 %copy-start.8 = (s32[16,8]{0,1:T(8,128)S(1)}, s32[16,8]{0,1:T(8,128)}, u32[]{:S(2)}) copy-start(s32[16,8]{0,1:T(8,128)} %param.28) | copy-start | bytes 1540
  6.5 32.4 %copy-start.15 = (s32[128]{0:T(128)S(1)}, s32[128]{0:T(128)}, u32[]{:S(2)}) copy-start(s32[128]{0:T(128)} %param.27) | copy-start | bytes 1540
  6.5 32.4 %copy-start.13 = (s32[4,4]{1,0:T(4,128)S(1)}, s32[4,4]{1,0:T(4,128)}, u32[]{:S(2)}) copy-start(s32[4,4]{1,0:T(4,128)} %param.25) | copy-start | bytes 196
  6.6 32.4 %copy-start.14 = (s32[128,4]{0,1:T(4,128)S(1)}, s32[128,4]{0,1:T(4,128)}, u32[]{:S(2)}) copy-start(s32[128,4]{0,1:T(4,128)} %param.26) | copy-start | bytes 6148
  6.6 50.2 %all-gather.4.cloned.1.call-start = ((), (), s32[]{:S(2)}) async-start(), calls=%async_computation.7 | async-start | bytes 1880064 | tf_op jit(solution)/shard_map/all_gather | solution.py:172
  7.3 74.4 %all-to-all-start.4 = ((bf16[8,144,360]{2,1,0:T(8,128)(2,1)}), bf16[8,144,360]{2,1,0:T(8,128)(2,1)S(1)}, u32[]{:S(2)}, u32[]{:S(2)}) async-start(bf16[8,144,360]{2,1,0:T(8,128)(2,1)} %param.23), calls=%async_computation.4 | async-start | bytes 1769472 | tf_op jit(solution)/shard_map/all_to_all | solution.py:164
  37.9 18.9 %copy-start.1 = (bf16[128,2304]{1,0:T(8,128)(2,1)}, bf16[128,2304]{1,0:T(8,128)(2,1)S(1)}, u32[]{:S(2)}) copy-start(bf16[128,2304]{1,0:T(8,128)(2,1)S(1)} %all_gather.12.tokens_ref) | copy-start | bytes 1769476
  95.1 3.7 %copy-start.9 = (s32[8,2]{0,1:T(2,128)S(1)}, s32[8,2]{0,1:T(2,128)}, u32[]{:S(2)}) copy-start(s32[8,2]{0,1:T(2,128)} %param.29) | copy-start | bytes 196
  95.1 5.6 %copy-start.4 = (bf16[128,144]{0,1:T(8,128)(2,1)S(1)}, bf16[128,144]{0,1:T(8,128)(2,1)}, u32[]{:S(2)}) copy-start(bf16[128,144]{0,1:T(8,128)(2,1)} %param.18) | copy-start | bytes 110596
  95.1 58.6 %copy-start.3 = (bf16[128,128]{1,0:T(8,128)(2,1)S(1)}, bf16[128,128]{1,0:T(8,128)(2,1)}, u32[]{:S(2)}) copy-start(bf16[128,128]{1,0:T(8,128)(2,1)} %attention.1) | copy-start | bytes 98308
  95.1 62.1 %all-to-all-start.3 = ((bf16[8,2,144,360]{3,1,2,0:T(2,128)(2,1)}), bf16[8,2,144,360]{3,1,2,0:T(2,128)(2,1)S(1)}, u32[]{:S(2)}, u32[]{:S(2)}) async-start(bf16[8,2,144,360]{3,1,2,0:T(2,128)(2,1)} %bitcast.61), calls=%async_computation.3 | async-start | bytes 3538944 | tf_op jit(solution)/shard_map/all_to_all | solution.py:164
  154.4 8.9 %copy-start.6 = (s32[8,16]{1,0:T(8,128)S(1)}, s32[8,16]{1,0:T(8,128)}, u32[]{:S(2)}) copy-start(s32[8,16]{1,0:T(8,128)} %get-tuple-element.5) | copy-start | bytes 1540
  154.4 9.4 %copy-start.16 = (s32[16]{0:T(128)S(1)}, s32[16]{0:T(128)}, u32[]{:S(2)}) copy-start(s32[16]{0:T(128)} %and_select_fusion) | copy-start | bytes 196
  154.5 9.5 %copy-start.12 = (bf16[2304]{0:T(1024)(128)(2,1)S(1)}, bf16[2304]{0:T(1024)(128)(2,1)}, u32[]{:S(2)}) copy-start(bf16[2304]{0:T(1024)(128)(2,1)} %param.20) | copy-start | bytes 13828
  154.5 20.6 %copy-start.5 = (s32[8,16]{1,0:T(8,128)S(1)}, s32[8,16]{1,0:T(8,128)}, u32[]{:S(2)}) copy-start(s32[8,16]{1,0:T(8,128)} %get-tuple-element.6) | copy-start | bytes 1540
  157.2 17.7 %all-to-all-start.1 = ((bf16[16,8,2304]{2,1,0:T(8,128)(2,1)}), bf16[16,8,2304]{2,1,0:T(8,128)(2,1)S(1)}, u32[]{:S(2)}, u32[]{:S(2)}) async-start(bf16[16,8,2304]{2,1,0:T(8,128)(2,1)} %fusion), calls=%async_computation.1 | async-start | bytes 1179648 | tf_op jit(solution)/shard_map/all_to_all | solution.py:202
  163.3 70.9 %all-gather.6.cloned.1.call-start = ((), (), s32[]{:S(2)}) async-start(), calls=%async_computation.8 | async-start | bytes 2506752 | tf_op jit(solution)/shard_map/all_gather | solution.py:237
  163.3 31.5 %collective-permute-start = (bf16[8,2,144,360]{3,1,2,0:T(2,128)(2,1)S(1)}, bf16[8,2,144,360]{3,1,2,0:T(2,128)(2,1)}, u32[]{:S(2)}, u32[]{:S(2)}) collective-permute-start(bf16[8,2,144,360]{3,1,2,0:T(2,128)(2,1)S(1)} %all-to-all-done.3), channel_id=1, source_target_pairs={{0,16},{16,0},{32,48},{48,32},{64,80},{80,64},{96,112},{112,96},{1... | collective-permute-start | bytes 4976648 | tf_op jit(solution)/shard_map/ppermute | solution.py:244
  164.0 27.6 %collective-permute-start.1 = (bf16[8,144,360]{2,1,0:T(8,128)(2,1)S(1)}, bf16[8,144,360]{2,1,0:T(8,128)(2,1)}, u32[]{:S(2)}, u32[]{:S(2)}) collective-permute-start(bf16[8,144,360]{2,1,0:T(8,128)(2,1)S(1)} %all-to-all-done.4), channel_id=1, source_target_pairs={{0,16},{16,0},{32,48},{48,32},{64,80},{80,64},{96,112},{112,96},{1... | collective-permute-start | bytes 2488328 | tf_op jit(solution)/shard_map/ppermute | solution.py:244
  247.7 4.9 %copy-start.10 = (s32[8,2]{0,1:T(2,128)S(1)}, s32[8,2]{0,1:T(2,128)}, u32[]{:S(2)}) copy-start(s32[8,2]{0,1:T(2,128)} %param.29) | copy-start | bytes 196
  247.7 35.9 %all-to-all-start.5 = ((bf16[16,32,2304]{2,1,0:T(8,128)(2,1)}), bf16[16,32,2304]{2,1,0:T(8,128)(2,1)S(1)}, u32[]{:S(2)}, u32[]{:S(2)}) async-start(bf16[16,32,2304]{2,1,0:T(8,128)(2,1)} %bitcast.60), calls=%async_computation.5 | async-start | bytes 4718592 | tf_op jit(solution)/shard_map/all_to_all | solution.py:258
  252.4 43.1 %copy-start.7 = (f32[16,8]{0,1:T(8,128)S(1)}, f32[16,8]{0,1:T(8,128)}, u32[]{:S(2)}) copy-start(f32[16,8]{0,1:T(8,128)} %get-tuple-element.29) | copy-start | bytes 1540
  284.7 20.0 %all-to-all-start.6 = ((bf16[16,2,2304]{2,1,0:T(2,128)(2,1)}), bf16[16,2,2304]{2,1,0:T(2,128)(2,1)S(1)}, u32[]{:S(2)}, u32[]{:S(2)}) async-start(bf16[16,2,2304]{2,1,0:T(2,128)(2,1)} %reshape.229), calls=%async_computation.6 | async-start | bytes 294912 | tf_op jit(solution)/shard_map/all_to_all | solution.py:266
Sparse Core Ops, SparseCore 0:
  9.3 47.5 all-gather.3
  191.7 42.4 all-gather.5

commit v2 on v1

--- a/solution.py
+++ b/solution.py
@@ -123,6 +123,73 @@
         limit,
         cache_pool.reshape(rows, width),
     )
+
+
+def exchange_kernel(axis, count, gather, reduce, src_ref, out_ref, *scratch):
+    land_ref = scratch[0] if reduce else out_ref
+    send_sem, recv_sem, own_sem = scratch[-3:]
+    me = lax.axis_index(axis)
+    barrier = pltpu.get_barrier_semaphore()
+    for step in range(1, count):
+        pl.semaphore_signal(
+            barrier,
+            inc=1,
+            device_id={axis: lax.rem(me + step, count)},
+            device_id_type=pl.DeviceIdType.MESH,
+        )
+    pl.semaphore_wait(barrier, count - 1)
+    copies = []
+    for step in range(1, count):
+        peer = lax.rem(me + step, count)
+        copy = pltpu.make_async_remote_copy(
+            src_ref=src_ref if gather else src_ref.at[peer],
+            dst_ref=land_ref.at[me],
+            send_sem=send_sem.at[step],
+            recv_sem=recv_sem.at[step],
+            device_id={axis: peer},
+            device_id_type=pl.DeviceIdType.MESH,
+        )
+        copy.start()
+        copies.append(copy)
+    own = pltpu.make_async_copy(src_ref if gather else src_ref.at[me], land_ref.at[me], own_sem)
+    own.start()
+    own.wait()
+    for copy in copies:
+        copy.wait()
+    if reduce:
+        width = land_ref.shape[2]
+        block = width // 6
+        for start in range(0, width, block):
+            total = land_ref[0, :, start : start + block].astype(F32)
+            for source in range(1, count):
+                total = total + land_ref[source, :, start : start + block].astype(F32)
+            out_ref[:, start : start + block] = total.astype(out_ref.dtype)
+
+
+def exchange(values, axis, number, name, gather=False, reduce=None):
+    count = lax.axis_size(axis)
+    block = values.shape if gather else values.shape[1:]
+    landing = (count,) + block
+    semaphores = [
+        pltpu.SemaphoreType.DMA((count,)),
+        pltpu.SemaphoreType.DMA((count,)),
+        pltpu.SemaphoreType.DMA,
+    ]
+    if reduce is None:
+        result = jax.ShapeDtypeStruct(landing, values.dtype)
+        scratch = semaphores
+    else:
+        result = jax.ShapeDtypeStruct(block, reduce)
+        scratch = [pltpu.VMEM(landing, values.dtype)] + semaphores
+    return pl.pallas_call(
+        functools.partial(exchange_kernel, axis, count, gather, reduce is not None),
+        out_shape=result,
+        in_specs=[vmem()],
+        out_specs=vmem(),
+        scratch_shapes=scratch,
+        compiler_params=pltpu.CompilerParams(collective_id=number, has_side_effects=True),
+        name=name,
+    )(values)
 
 
 def local(
@@ -165,12 +232,22 @@
             values, "dp", split_axis=0, concat_axis=0, tiled=True, axis_index_groups=same_core
         )
 
-    gate_half = spread_weights(jnp.transpose(gate_up, (0, 2, 1, 3)))
-    down_half = spread_weights(expert_down)
-
-    row_tokens = lax.all_gather(hidden_in, "fsdp", axis=0, tiled=True)
-    weight_in = lax.all_gather(jnp.transpose(project_in, (1, 0, 2)), "dp", axis=1, tiled=True)
-    weight_out = lax.all_gather(project_out.T, "dp", axis=0, tiled=True)
+    row_tokens = exchange(hidden_in, "fsdp", 0, "row_tokens", gather=True)
+    row_tokens = row_tokens.reshape(req_row, model_width)
+    weights = jnp.concatenate(
+        [jnp.transpose(project_in, (1, 0, 2)), project_out.T[None]], axis=0
+    )
+    weights = lax.all_gather(weights, "dp", axis=1, tiled=True)
+    weight_in, weight_out = weights[:3], weights[3]
+    gate_up, expert_down, weights = lax.optimization_barrier((gate_up, expert_down, weights))
+    gate_own = spread_weights(
+        gate_up.reshape(expert_count, features_here, 2 * units_here)
+    ).reshape(-1, 2 * units_here)
+    down_own = spread_weights(expert_down).reshape(-1, units_here)
+    swap = [(d, d ^ 1) for d in range(rows_count)]
+    gate_other = lax.ppermute(gate_own, "dp", swap)
+    down_other = lax.ppermute(down_own, "dp", swap)
+
     group_hit = (
         groups[:, None] == jnp.arange(prompt_pages.shape[0], dtype=jnp.int32)[None, :]
     ).astype(jnp.int32)
@@ -189,7 +266,7 @@
     send_select = (move_target[my_row][None, :] == row_numbers[:, None]).astype(BF16)
     leaving = jnp.concatenate([heads_out[staying:], row_tokens[staying:]], axis=1)
     leaving_send = jnp.dot(send_select, leaving, preferred_element_type=F32).astype(BF16)
-    leaving_recv = lax.all_to_all(leaving_send, "dp", split_axis=0, concat_axis=0, tiled=True)
+    leaving_recv = exchange(leaving_send[:, None, :], "dp", 1, "leaving")[:, 0]
     arrive_select = (move_target == my_row).astype(BF16)
     arrived = lax.dot_general(
         arrive_select, leaving_recv, (((0,), (0,)), ((), ())), preferred_element_type=F32
@@ -199,14 +276,13 @@
         my_column == fsdp_count - 1, arrived[:, head_cols:], hidden_in
     )
     partial_out = dot_t(heads_row, weight_out).astype(BF16)
-    partial_recv = lax.all_to_all(
+    attn_proj = exchange(
         partial_out.reshape(fsdp_count, req_local, model_width),
         "fsdp",
-        split_axis=0,
-        concat_axis=0,
-        tiled=True,
-    )
-    attn_proj = jnp.sum(partial_recv.astype(F32), axis=0)
+        2,
+        "partial_out",
+        reduce=F32,
+    )
     resid = mine_tokens.astype(F32) + attn_proj
     moe_in = rms_scale(resid, norm_second).astype(BF16)
     logits = jnp.dot(moe_in, router, preferred_element_type=F32)
@@ -233,47 +309,57 @@
     dispatch = jnp.einsum(
         "dst,tm->dsm", select.astype(BF16), moe_in, preferred_element_type=F32
     ).astype(BF16)
-    received = lax.all_to_all(dispatch, "dp", split_axis=0, concat_axis=0, tiled=True)
-    expert_tokens = lax.all_gather(received[None], "fsdp", axis=0, tiled=True)
+    by_core = dispatch.reshape(rows_count // 2, 2, slots_row, rows_count // 2, 2, features_here)
+    half = model_width // 2
+    cores = [by_core[:, :, :, :, c].reshape(rows_count // 2, 2, slots_row, half) for c in range(2)]
+    dispatch = jnp.stack(
+        [
+            jnp.concatenate([cores[0][:, 0], cores[1][:, 0]], axis=-1),
+            jnp.concatenate([cores[1][:, 1], cores[0][:, 1]], axis=-1),
+        ],
+        axis=1,
+    ).reshape(rows_count, slots_row, model_width)
+    received = exchange(dispatch, "dp", 3, "dispatch")
+    expert_tokens = exchange(
+        received.reshape(rows_count * slots_row, model_width), "fsdp", 4, "expert_tokens", gather=True
+    )
     flattened = expert_tokens.reshape(-1, model_width)
-
-    swap = [(d, d ^ 1) for d in range(rows_count)]
-    first_core = my_row % 2 == 0
-
-    def both(values):
-        other = lax.ppermute(values, "dp", swap)
-        return jnp.stack(
-            [jnp.where(first_core, values, other), jnp.where(first_core, other, values)], axis=1
-        )
-
-    gate_whole = both(gate_half)
-    down_whole = both(down_half)
-    down_cols = down_whole.reshape(model_width, units_here)
-    gate_cols = gate_whole[:, :, 0].reshape(model_width, units_here)
-    up_cols = gate_whole[:, :, 1].reshape(model_width, units_here)
-    gate_part = jnp.dot(flattened, gate_cols, preferred_element_type=F32)
-    up_part = jnp.dot(flattened, up_cols, preferred_element_type=F32)
-    activation = (jax.nn.silu(gate_part) * up_part).astype(BF16)
-    expert_y = dot_t(activation, down_cols).astype(BF16)
-    returned = lax.all_to_all(
+    gate_up_part = jnp.dot(
+        flattened[:, :half], gate_own, preferred_element_type=F32
+    ) + jnp.dot(flattened[:, half:], gate_other, preferred_element_type=F32)
+    activation = (
+        jax.nn.silu(gate_up_part[:, :units_here]) * gate_up_part[:, units_here:]
+    ).astype(BF16)
+    expert_y = jnp.concatenate(
+        [dot_t(activation, down_own).astype(BF16), dot_t(activation, down_other).astype(BF16)],
+        axis=1,
+    )
+    returned = exchange(
         expert_y.reshape(fsdp_count, rows_count * slots_row, model_width),
         "fsdp",
-        split_axis=0,
-        concat_axis=0,
-        tiled=True,
-    )
-    returned = jnp.sum(returned.astype(F32), axis=0).astype(BF16)
-    back_rows = lax.all_to_all(
-        returned.reshape(rows_count, slots_row, model_width),
-        "dp",
-        split_axis=0,
-        concat_axis=0,
-        tiled=True,
+        5,
+        "expert_sums",
+        reduce=BF16,
+    )
+    back_rows = exchange(
+        returned.reshape(rows_count, slots_row, model_width), "dp", 6, "back_rows"
     )
     coefficient = select.astype(F32) * mix_row.T[:, None, :]
-    moe_total = jnp.einsum(
-        "dst,dsm->tm", coefficient, back_rows.astype(F32), precision=lax.Precision.HIGHEST
-    )
+    coefficient = coefficient.reshape(rows_count // 2, 2, slots_row, req_local)
+    back_rows = back_rows.astype(F32).reshape(rows_count // 2, 2, slots_row, model_width)
+    sums = [
+        jnp.einsum(
+            "dst,dsm->tm", coefficient[:, c], back_rows[:, c], precision=lax.Precision.HIGHEST
+        )
+        for c in range(2)
+    ]
+    by_core = [
+        sums[0][:, :half] + sums[1][:, half:],
+        sums[0][:, half:] + sums[1][:, :half],
+    ]
+    moe_total = jnp.stack(
+        [part.reshape(req_local, rows_count // 2, features_here) for part in by_core], axis=2
+    ).reshape(req_local, model_width)
     return (resid + moe_total).astype(BF16)
 
 

time: 313 us -> 309 us (0.987)
  Pallas kernels: 22.6 us -> 220 us
  blocking collectives: 103 us -> 0 us
  waiting for transfers between devices: 92.3 us -> 19.3 us
  starting transfers between devices: 34.9 us -> 10.1 us
  local copies, waits for them, and re-layouts: 13.3 us -> 21.2 us
  other arithmetic: 19.5 us -> 12.6 us
    pallas_call x0 -> x7, Pallas kernels: none -> 197 us  [exchange(): pl.pallas_call(functools.partial(exchange_kernel, axis, count, gather, re...]
    all_gather x2 -> x0, blocking collectives: 73.9 us -> none  [the longest x1 52.9 us: local(): weight_out = lax.all_gather(project_out.T, 'dp', axis=0, tiled=True)]
    all_to_all x3 -> x0, waiting for transfers between devices: 50.8 us -> none  [the longest x1 30.8 us: local(): lax.all_to_all(expert_y.reshape(fsdp_count, rows_count * slots_row, model...]
    all_to_all x2 -> x0, blocking collectives: 29.5 us -> none  [the longest x1 16.1 us: local(): lax.all_to_all(dispatch, 'dp', split_axis=0, concat_axis=0, tiled=True)]
    all_gather x2 -> x1, waiting for transfers between devices: 40.8 us -> 19.2 us  [local(): weights = lax.all_gather(weights, 'dp', axis=1, tiled=True)]
    all_to_all x3 -> x0, starting transfers between devices: 21.4 us -> none  [the longest x1 10.7 us: local(): lax.all_to_all(returned.reshape(rows_count, slots_row, model_width), 'dp'...]
    another operation x4, other arithmetic: 13 us -> 1.11 us  [the longest x3 0.98 us: local(): jnp.stack([jnp.concatenate([cores[0][:, 0], cores[1][:, 0]], axis=-1), jn...]
    all_to_all x2, starting transfers between devices: 12.8 us -> 7.63 us  [spread_weights(): lax.all_to_all(values, 'dp', split_axis=0, concat_axis=0, tiled=True, axi...]
  transfers between devices with their start and end apart: 9 -> 5, of which waited for: 5 -> 1; matrix products, arithmetic and copies ran while one was open for 10% -> 10% of each run, Pallas kernels for 7% -> 47%
where the time goes in v2:
time: 309 us; the launch traced here: 308 us
  Pallas kernels  220 us (71%)
  local copies, waits for them, and re-layouts  21.2 us (7%)
  waiting for transfers between devices  19.3 us (6%)
  between operations  13.8 us (4%)
  other arithmetic  12.6 us (4%)
  matrix products  11.2 us (4%)
  starting transfers between devices  10.1 us (3%)
    pallas_call x7, Pallas kernels, exchange(): pl.pallas_call(functools.partial(exchange_kernel, axis, count, gather, re...  197 us
    pallas_call x1, Pallas kernels, attention(): pl.pallas_call(functools.partial(attention_kernel, page_len), out_shape=j...  22.7 us
    all_gather x1, waiting for transfers between devices, local(): weights = lax.all_gather(weights, 'dp', axis=1, tiled=True)  19.2 us
    all_to_all x2, starting transfers between devices, spread_weights(): lax.all_to_all(values, 'dp', split_axis=0, concat_axis=0, tiled=True, axi...  7.63 us
  transfers between devices with their start and end apart: 5, of which 1 were waited for; matrix products, arithmetic and copies ran while one was open for 10% of the time, Pallas kernels for 47%

profile of v2, /device:TPU:1, one launch (start us, length us, event | category | flops | bytes accessed | tf_op | source)
XLA Modules:
  0.0 308.0 jit_solution(9271103980375602145)
XLA Ops:
  6.5 1.6 pad_maximum_fusion.1
  8.2 16.0 %row_tokens.1 = bf16[16,8,2304]{2,1,0:T(8,128)(2,1)} custom-call(bf16[8,2304]{1,0:T(8,128)(2,1)} %src_ref.1), custom_call_target="tpu_custom_call" | custom-call | tf_op jit(solution)/shard_map/row_tokens/pallas_call | solution.py:184
  24.2 1.3 broadcast_in_dim.126.norm_ref
  31.4 1.0 fusion.8
  32.4 1.1 select_add_fusion.limit_ref
  34.2 19.2 %all-gather.2.cloned.1.call-done = bf16[4,2304,128]{2,1,0:T(8,128)(2,1)} async-done(((bf16[4,144,128]{2,1,0:T(8,128)(2,1)}), bf16[4,2304,128]{2,1,0:T(8,128)(2,1)}) %all-gather.2.cloned.1.call-update) | async-done | bytes 2359312 | tf_op jit(solution)/shard_map/all_gather | solution.py:240
  53.4 2.8 slice.146.weight_ref
  56.2 22.7 %attention.1 = bf16[128,128]{1,0:T(8,128)(2,1)} custom-call(bf16[128,2304]{1,0:T(8,128)(2,1)} %bitcast.106, bf16[1,2304]{1,0:T(2,128)(2,1)} %broadcast_in_dim.126.norm_ref, bf16[3,2304,128]{2,1,0:T(8,128)(2,1)} %slice.146.weight_ref, f32[128,128]{1,0:T(8,128)} %get-tuple-element.36.cos_ref, f32[128,128]{1,0:T(8,128)} %get-tuple-element.35.sin_ref, ...), custom_call_target="tpu_custom_call" | custom-call | tf_op jit(solution)/shard_map/attention/pallas_call | solution.py:106
  78.9 2.6 reshape.272
  81.5 4.1 %all-to-all-start = ((bf16[8,144,720]{2,1,0:T(8,128)(2,1)}), bf16[8,144,720]{2,1,0:T(8,128)(2,1)S(1)}, u32[]{:S(2)}, u32[]{:S(2)}) async-start(bf16[8,144,720]{2,1,0:T(8,128)(2,1)} %reshape.272), calls=%async_computation | async-start | bytes 3538944 | tf_op jit(solution)/shard_map/all_to_all | solution.py:231
  86.5 46.9 %leaving.1 = bf16[16,1,2432]{2,1,0:T(2,128)(2,1)} custom-call(bf16[16,1,2432]{2,1,0:T(2,128)(2,1)} %copy.85.src_ref), custom_call_target="tpu_custom_call" | custom-call | tf_op jit(solution)/shard_map/leaving/pallas_call | solution.py:184
  133.5 1.0 convolution_convert_fusion.3
  134.5 2.2 fusion.src_ref
  136.7 15.0 %partial_out.1 = f32[8,2304]{1,0:T(8,128)} custom-call(bf16[16,8,2304]{2,1,0:T(8,128)(2,1)} %fusion.src_ref), custom_call_target="tpu_custom_call" | custom-call | tf_op jit(solution)/shard_map/partial_out/pallas_call | solution.py:184
  151.7 1.0 multiply_reduce_fusion
  153.5 1.1 slice_reduce_fusion
  155.6 3.6 %all-to-all-start.1 = ((bf16[8,144,360]{2,1,0:T(8,128)(2,1)}), bf16[8,144,360]{2,1,0:T(8,128)(2,1)S(1)}, u32[]{:S(2)}, u32[]{:S(2)}) async-start(bf16[8,144,360]{2,1,0:T(8,128)(2,1)} %param.23), calls=%async_computation.1 | async-start | bytes 1769472 | tf_op jit(solution)/shard_map/all_to_all | solution.py:231
  159.2 2.3 copy.95
  161.5 1.2 collective-permute-start
  163.5 24.7 %dispatch.1 = bf16[16,2,2304]{2,1,0:T(2,128)(2,1)} custom-call(bf16[16,2,2304]{2,1,0:T(2,128)(2,1)} %bitcast.110), custom_call_target="tpu_custom_call" | custom-call | tf_op jit(solution)/shard_map/dispatch/pallas_call | solution.py:184
  188.3 1.6 reshape.270.src_ref
  189.9 40.8 %expert_tokens.1 = bf16[16,32,2304]{2,1,0:T(8,128)(2,1)} custom-call(bf16[32,2304]{1,0:T(8,128)(2,1)} %reshape.270.src_ref), custom_call_target="tpu_custom_call" | custom-call | tf_op jit(solution)/shard_map/expert_tokens/pallas_call | solution.py:184
  231.5 1.5 copy.96
  233.0 1.2 collective-permute-start.1
  234.2 2.6 fusion.3
  236.8 2.6 convolution_add_fusion
  239.7 0.9 convolution_convert_fusion.4
  241.4 1.6 pad_maximum_fusion
  243.0 42.1 %expert_sums.1 = bf16[32,2304]{1,0:T(8,128)(2,1)} custom-call(bf16[16,32,2304]{2,1,0:T(8,128)(2,1)} %bitcast.100), custom_call_target="tpu_custom_call" | custom-call | tf_op jit(solution)/shard_map/expert_sums/pallas_call | solution.py:184
  285.2 1.6 reshape.276.src_ref
  286.8 11.6 %back_rows.1 = bf16[16,2,2304]{2,1,0:T(2,128)(2,1)} custom-call(bf16[16,2,2304]{2,1,0:T(2,128)(2,1)} %reshape.276.src_ref), custom_call_target="tpu_custom_call" | custom-call | tf_op jit(solution)/shard_map/back_rows/pallas_call | solution.py:184
  298.4 1.0 fusion.33
  (84 shorter events, 13.7 us)
Async XLA Ops:
  6.5 224.2 %copy-start = (bf16[2304,8]{0,1:T(8,128)(2,1)S(1)}, bf16[2304,8]{0,1:T(8,128)(2,1)}, u32[]{:S(2)}) copy-start(bf16[2304,8]{0,1:T(8,128)(2,1)} %param.21) | copy-start | bytes 110596
  6.5 46.9 %all-gather.2.cloned.1.call-start = ((), (), s32[]{:S(2)}) async-start(), calls=%async_computation.2 | async-start | bytes 2506752 | tf_op jit(solution)/shard_map/all_gather | solution.py:240
  56.2 22.7 %copy-start.2 = (bf16[8,144,2,360]{3,2,1,0:T(2,128)(2,1)S(1)}, bf16[8,144,2,360]{3,2,1,0:T(2,128)(2,1)}, u32[]{:S(2)}) copy-start(bf16[8,144,2,360]{3,2,1,0:T(2,128)(2,1)} %param.22) | copy-start | bytes 4976644
  81.5 4.1 %slice-start = ((bf16[128,128]{1,0:T(8,128)(2,1)}), bf16[8,128]{1,0:T(8,128)(2,1)S(1)}, s32[]{:S(2)}) async-start(bf16[128,128]{1,0:T(8,128)(2,1)} %attention.1), calls=%async_computation.3 | async-start | bytes 4096 | tf_op jit(solution)/shard_map/slice | solution.py:267
  81.5 51.9 %copy-start.4 = (s32[16,8]{0,1:T(8,128)S(1)}, s32[16,8]{0,1:T(8,128)}, u32[]{:S(2)}) copy-start(s32[16,8]{0,1:T(8,128)} %param.28) | copy-start | bytes 1540
  81.5 53.0 %slice-start.1 = ((bf16[128,128]{1,0:T(8,128)(2,1)}), bf16[120,128]{1,0:T(8,128)(2,1)S(1)}, s32[]{:S(2)}) async-start(bf16[128,128]{1,0:T(8,128)(2,1)} %attention.1), calls=%async_computation.4 | async-start | bytes 61440 | tf_op jit(solution)/shard_map/slice | solution.py:274
  81.5 74.1 %all-to-all-start = ((bf16[8,144,720]{2,1,0:T(8,128)(2,1)}), bf16[8,144,720]{2,1,0:T(8,128)(2,1)S(1)}, u32[]{:S(2)}, u32[]{:S(2)}) async-start(bf16[8,144,720]{2,1,0:T(8,128)(2,1)} %reshape.272), calls=%async_computation | async-start | bytes 3538944 | tf_op jit(solution)/shard_map/all_to_all | solution.py:231
  85.6 66.1 %copy-start.3 = (bf16[8,2304]{1,0:T(8,128)(2,1)S(1)}, bf16[8,2304]{1,0:T(8,128)(2,1)}, u32[]{:S(2)}) copy-start(bf16[8,2304]{1,0:T(8,128)(2,1)} %src_ref.1) | copy-start | bytes 110596
  155.6 75.9 %all-to-all-start.1 = ((bf16[8,144,360]{2,1,0:T(8,128)(2,1)}), bf16[8,144,360]{2,1,0:T(8,128)(2,1)S(1)}, u32[]{:S(2)}, u32[]{:S(2)}) async-start(bf16[8,144,360]{2,1,0:T(8,128)(2,1)} %param.23), calls=%async_computation.1 | async-start | bytes 1769472 | tf_op jit(solution)/shard_map/all_to_all | solution.py:231
  161.5 69.5 %copy-start.5 = (s32[8,2]{0,1:T(2,128)S(1)}, s32[8,2]{0,1:T(2,128)}, u32[]{:S(2)}) copy-start(s32[8,2]{0,1:T(2,128)} %param.29) | copy-start | bytes 196
  161.5 75.3 %collective-permute-start = (bf16[1152,720]{0,1:T(8,128)(2,1)}, bf16[1152,720]{0,1:T(8,128)(2,1)}, u32[]{:S(2)}, u32[]{:S(2)}) collective-permute-start(bf16[1152,720]{0,1:T(8,128)(2,1)} %copy.95), channel_id=1, source_target_pairs={{0,16},{16,0},{32,48},{48,32},{64,80},{80,64},{96,112},{112,96},{1... | collective-permute-start | bytes 4976648 | tf_op jit(solution)/shard_map/ppermute | solution.py:248
  233.0 7.6 %collective-permute-start.1 = (bf16[1152,360]{0,1:T(8,128)(2,1)}, bf16[1152,360]{0,1:T(8,128)(2,1)S(1)}, u32[]{:S(2)}, u32[]{:S(2)}) collective-permute-start(bf16[1152,360]{0,1:T(8,128)(2,1)} %copy.96), channel_id=1, source_target_pairs={{0,16},{16,0},{32,48},{48,32},{64,80},{80,64},{96,112},{112,96},{1... | collective-permute-start | bytes 2488328 | tf_op jit(solution)/shard_map/ppermute | solution.py:249
  234.2 2.6 copy-start.1
Sparse Core Ops, SparseCore 0:
  9.2 44.1 all-gather.1

commit v3 on v2

--- a/solution.py
+++ b/solution.py
@@ -113,6 +113,9 @@
             pltpu.VMEM((page_len, count * (width // HD), pages), F32),
         ],
         compiler_params=pltpu.CompilerParams(vmem_limit_bytes=56 * 1024 * 1024),
+        cost_estimate=pl.CostEstimate(
+            flops=4 * count * width * rows, bytes_accessed=60_000_000, transcendentals=0
+        ),
         name="attention",
     )(
         tokens,
@@ -188,8 +191,225 @@
         out_specs=vmem(),
         scratch_shapes=scratch,
         compiler_params=pltpu.CompilerParams(collective_id=number, has_side_effects=True),
+        cost_estimate=pl.CostEstimate(flops=0, bytes_accessed=200_000_000, transcendentals=0),
         name=name,
     )(values)
+
+
+def torus_ids(axis, side):
+    me = lax.axis_index(axis)
+    y, x = me // side, lax.rem(me, side)
+
+    def peer(along_y, step):
+        if along_y:
+            return {axis: lax.rem(y + step, side) * side + x}
+        return {axis: y * side + lax.rem(x + step, side)}
+
+    return y, x, peer
+
+
+def torus_barrier(peer, side):
+    barrier = pltpu.get_barrier_semaphore()
+    for along_y in (False, True):
+        for step in range(1, side):
+            pl.semaphore_signal(
+                barrier,
+                inc=1,
+                device_id=peer(along_y, step),
+                device_id_type=pl.DeviceIdType.MESH,
+            )
+    pl.semaphore_wait(barrier, 2 * (side - 1))
+
+
+def torus_gather_kernel(axis, side, src_ref, out_ref, send_sem, recv_sem, own_sem):
+    y, x, peer = torus_ids(axis, side)
+    half = src_ref.shape[0] // 2
+    rows = [pl.ds(0, half), pl.ds(half, half)]
+    part = [pl.ds(0, side // 2), pl.ds(side // 2, side - side // 2)]
+    torus_barrier(peer, side)
+
+    def send(h, number, src, dst, device):
+        copy = pltpu.make_async_remote_copy(
+            src_ref=src,
+            dst_ref=dst,
+            send_sem=send_sem.at[h, number],
+            recv_sem=recv_sem.at[h, number],
+            device_id=device,
+            device_id_type=pl.DeviceIdType.MESH,
+        )
+        copy.start()
+        return copy
+
+    first = [
+        [
+            send(h, step - 1, src_ref.at[rows[h]], out_ref.at[y, x, rows[h]], peer(h == 1, step))
+            for step in range(1, side)
+        ]
+        for h in range(2)
+    ]
+    own = pltpu.make_async_copy(src_ref, out_ref.at[y, x], own_sem)
+    own.start()
+    own.wait()
+
+    def group(h, step, blocks):
+        if h == 0:
+            return out_ref.at[lax.rem(y + step, side), blocks, rows[h]]
+        return out_ref.at[blocks, lax.rem(x + step, side), rows[h]]
+
+    whole = pl.ds(0, side)
+    second = []
+    for h in range(2):
+        for copy in first[h]:
+            copy.wait()
+        second.append(
+            [
+                send(h, 3, group(h, 0, whole), group(h, 0, whole), peer(h == 0, 1)),
+                send(h, 4, group(h, 0, whole), group(h, 0, whole), peer(h == 0, side - 1)),
+            ]
+        )
+    third = []
+    for h in range(2):
+        for k, back in ((0, side - 1), (1, 1)):
+            second[h][k].wait()
+            source = group(h, back, part[k])
+            third.append(send(h, 5 + k, source, source, peer(h == 0, side - back)))
+    for copy in third:
+        copy.wait()
+
+
+def torus_gather(values, axis, number, name):
+    count = lax.axis_size(axis)
+    side = 4
+    return pl.pallas_call(
+        functools.partial(torus_gather_kernel, axis, side),
+        out_shape=jax.ShapeDtypeStruct((side, count // side) + values.shape, values.dtype),
+        in_specs=[vmem()],
+        out_specs=vmem(),
+        scratch_shapes=[
+            pltpu.SemaphoreType.DMA((2, 7)),
+            pltpu.SemaphoreType.DMA((2, 7)),
+            pltpu.SemaphoreType.DMA,
+        ],
+        compiler_params=pltpu.CompilerParams(collective_id=number, has_side_effects=True),
+        cost_estimate=pl.CostEstimate(flops=0, bytes_accessed=60_000_000, transcendentals=0),
+        name=name,
+    )(values)
+
+
+def torus_sum_kernel(
+    axis, side, src_ref, out_ref, land_ref, relay_ref, sum_ref, last_ref, send_sem, recv_sem
+):
+    y, x, peer = torus_ids(axis, side)
+    half = src_ref.shape[2] // 2
+    width = src_ref.shape[3]
+    block = width // 3
+    rows = [pl.ds(0, half), pl.ds(half, half)]
+    part = [pl.ds(0, side // 2), pl.ds(side // 2, side - side // 2)]
+    whole = pl.ds(0, side)
+    torus_barrier(peer, side)
+
+    def send(h, number, src, dst, device):
+        copy = pltpu.make_async_remote_copy(
+            src_ref=src,
+            dst_ref=dst,
+            send_sem=send_sem.at[h, number],
+            recv_sem=recv_sem.at[h, number],
+            device_id=device,
+            device_id_type=pl.DeviceIdType.MESH,
+        )
+        copy.start()
+        return copy
+
+    def terms(h, step, blocks):
+        if h == 0:
+            return src_ref.at[blocks, lax.rem(x + step, side), rows[h]]
+        return src_ref.at[lax.rem(y + step, side), blocks, rows[h]]
+
+    far, near, relays = [], [], []
+    for h in range(2):
+        far.append(
+            [
+                send(h, 0, terms(h, 2, part[0]), relay_ref.at[h, 0], peer(h == 1, 1)),
+                send(h, 1, terms(h, 2, part[1]), relay_ref.at[h, 1], peer(h == 1, side - 1)),
+            ]
+        )
+    for h in range(2):
+        near.append(
+            [
+                send(h, 2, terms(h, 1, whole), land_ref.at[h, 0], peer(h == 1, 1)),
+                send(h, 3, terms(h, side - 1, whole), land_ref.at[h, 2], peer(h == 1, side - 1)),
+            ]
+        )
+    for h in range(2):
+        for k, step in ((0, 1), (1, side - 1)):
+            far[h][k].wait()
+            relays.append(
+                send(
+                    h, 4 + k, relay_ref.at[h, k], land_ref.at[h, 1, part[k]], peer(h == 1, step)
+                )
+            )
+    for h in range(2):
+        for copy in near[h]:
+            copy.wait()
+    for copy in relays:
+        copy.wait()
+    last = []
+    for h in range(2):
+        for b in range(side):
+            for start in range(0, width, block):
+                cols = slice(start, start + block)
+                if h == 0:
+                    total = src_ref[b, x, 0:half, cols].astype(F32)
+                else:
+                    total = src_ref[y, b, half : 2 * half, cols].astype(F32)
+                for k in range(side - 1):
+                    total = total + land_ref[h, k, b, :, cols].astype(F32)
+                sum_ref[h, b, :, cols] = total.astype(sum_ref.dtype)
+        mine = y if h == 0 else x
+        for step in range(1, side):
+            last.append(
+                send(
+                    h,
+                    5 + step,
+                    sum_ref.at[h, lax.rem(mine + step, side)],
+                    last_ref.at[h, step - 1],
+                    peer(h == 0, step),
+                )
+            )
+    for copy in last:
+        copy.wait()
+    for h in range(2):
+        mine = y if h == 0 else x
+        for start in range(0, width, block):
+            cols = slice(start, start + block)
+            total = sum_ref[h, mine, :, cols].astype(F32)
+            for k in range(side - 1):
+                total = total + last_ref[h, k, :, cols].astype(F32)
+            out_ref[h * half : (h + 1) * half, cols] = total.astype(out_ref.dtype)
+
+
+def torus_sum(values, axis, number, name):
+    count, rows, width = values.shape
+    side = 4
+    half = rows // 2
+    return pl.pallas_call(
+        functools.partial(torus_sum_kernel, axis, side),
+        out_shape=jax.ShapeDtypeStruct((rows, width), values.dtype),
+        in_specs=[vmem()],
+        out_specs=vmem(),
+        scratch_shapes=[
+            pltpu.VMEM((2, side - 1, side, half, width), values.dtype),
+            pltpu.VMEM((2, 2, side // 2, half, width), values.dtype),
+            pltpu.VMEM((2, side, half, width), values.dtype),
+            pltpu.VMEM((2, side - 1, half, width), values.dtype),
+            pltpu.SemaphoreType.DMA((2, 9)),
+            pltpu.SemaphoreType.DMA((2, 9)),
+        ],
+        compiler_params=pltpu.CompilerParams(
+            collective_id=number, has_side_effects=True, vmem_limit_bytes=40 * 1024 * 1024
+        ),
+        name=name,
+    )(values.reshape(side, count // side, rows, width))
 
 
 def local(
@@ -239,14 +459,11 @@
     )
     weights = lax.all_gather(weights, "dp", axis=1, tiled=True)
     weight_in, weight_out = weights[:3], weights[3]
-    gate_up, expert_down, weights = lax.optimization_barrier((gate_up, expert_down, weights))
-    gate_own = spread_weights(
-        gate_up.reshape(expert_count, features_here, 2 * units_here)
-    ).reshape(-1, 2 * units_here)
-    down_own = spread_weights(expert_down).reshape(-1, units_here)
+    gate_cols, up_cols = gate_up[:, :, 0], gate_up[:, :, 1]
+    row_tokens, gate_cols, up_cols = lax.optimization_barrier((row_tokens, gate_cols, up_cols))
+    expert_down, weights = lax.optimization_barrier((expert_down, weights))
     swap = [(d, d ^ 1) for d in range(rows_count)]
-    gate_other = lax.ppermute(gate_own, "dp", swap)
-    down_other = lax.ppermute(down_own, "dp", swap)
+    down_own = spread_weights(expert_down)
 
     group_hit = (
         groups[:, None] == jnp.arange(prompt_pages.shape[0], dtype=jnp.int32)[None, :]
@@ -266,7 +483,12 @@
     send_select = (move_target[my_row][None, :] == row_numbers[:, None]).astype(BF16)
     leaving = jnp.concatenate([heads_out[staying:], row_tokens[staying:]], axis=1)
     leaving_send = jnp.dot(send_select, leaving, preferred_element_type=F32).astype(BF16)
+    leaving_send, down_own = lax.optimization_barrier((leaving_send, down_own))
+    down_own = down_own.reshape(-1, units_here)
     leaving_recv = exchange(leaving_send[:, None, :], "dp", 1, "leaving")[:, 0]
+    leaving_recv, gate_cols = lax.optimization_barrier((leaving_recv, gate_cols))
+    down_other = lax.ppermute(down_own, "dp", swap)
+    gate_own = spread_weights(gate_cols)
     arrive_select = (move_target == my_row).astype(BF16)
     arrived = lax.dot_general(
         arrive_select, leaving_recv, (((0,), (0,)), ((), ())), preferred_element_type=F32
@@ -285,6 +507,7 @@
     )
     resid = mine_tokens.astype(F32) + attn_proj
     moe_in = rms_scale(resid, norm_second).astype(BF16)
+    moe_in, gate_own = lax.optimization_barrier((moe_in, gate_own))
     logits = jnp.dot(moe_in, router, preferred_element_type=F32)
     expert_ids = jnp.arange(expert_count, dtype=jnp.int32)
     picked = routes[:, :, None] == expert_ids[None, None, :]
@@ -319,27 +542,32 @@
         ],
         axis=1,
     ).reshape(rows_count, slots_row, model_width)
+    gate_own = gate_own.reshape(-1, units_here)
     received = exchange(dispatch, "dp", 3, "dispatch")
-    expert_tokens = exchange(
-        received.reshape(rows_count * slots_row, model_width), "fsdp", 4, "expert_tokens", gather=True
+    received, up_cols = lax.optimization_barrier((received, up_cols))
+    gate_other = lax.ppermute(gate_own, "dp", swap)
+    up_own = spread_weights(up_cols).reshape(-1, units_here)
+    up_other = lax.ppermute(up_own, "dp", swap)
+    expert_tokens = torus_gather(
+        received.reshape(rows_count * slots_row, model_width), "fsdp", 4, "expert_tokens"
     )
     flattened = expert_tokens.reshape(-1, model_width)
-    gate_up_part = jnp.dot(
-        flattened[:, :half], gate_own, preferred_element_type=F32
-    ) + jnp.dot(flattened[:, half:], gate_other, preferred_element_type=F32)
-    activation = (
-        jax.nn.silu(gate_up_part[:, :units_here]) * gate_up_part[:, units_here:]
-    ).astype(BF16)
+    gate_part = jnp.dot(flattened[:, :half], gate_own, preferred_element_type=F32) + jnp.dot(
+        flattened[:, half:], gate_other, preferred_element_type=F32
+    )
+    up_part = jnp.dot(flattened[:, :half], up_own, preferred_element_type=F32) + jnp.dot(
+        flattened[:, half:], up_other, preferred_element_type=F32
+    )
+    activation = (jax.nn.silu(gate_part) * up_part).astype(BF16)
     expert_y = jnp.concatenate(
         [dot_t(activation, down_own).astype(BF16), dot_t(activation, down_other).astype(BF16)],
         axis=1,
     )
-    returned = exchange(
+    returned = torus_sum(
         expert_y.reshape(fsdp_count, rows_count * slots_row, model_width),
         "fsdp",
         5,
         "expert_sums",
-        reduce=BF16,
     )
     back_rows = exchange(
         returned.reshape(rows_count, slots_row, model_width), "dp", 6, "back_rows"

time: 309 us -> 243 us (0.79)
  Pallas kernels: 220 us -> 138 us
  waiting for transfers between devices: 19.3 us -> 26.6 us
  starting transfers between devices: 10.1 us -> 15.9 us
  other arithmetic: 12.6 us -> 8.38 us
  local copies, waits for them, and re-layouts: 21.2 us -> 24.3 us
    pallas_call x7 -> x5, Pallas kernels: 197 us -> 69.7 us  [exchange(): pl.pallas_call(functools.partial(exchange_kernel, axis, count, gather, re...]
    pallas_call x0 -> x2, Pallas kernels: none -> 46 us  [the longest x1 25.4 us: torus_gather(): pl.pallas_call(functools.partial(torus_gather_kernel, axis, side), out_sh...]
    all_to_all x2 -> x3, waiting for transfers between devices: 0.01 us -> 6.94 us  [spread_weights(): lax.all_to_all(values, 'dp', split_axis=0, concat_axis=0, tiled=True, axi...]
    all_to_all x2 -> x3, starting transfers between devices: 7.63 us -> 14.1 us  [spread_weights(): lax.all_to_all(values, 'dp', split_axis=0, concat_axis=0, tiled=True, axi...]
    slice x0 -> x1, local copies, waits for them, and re-layouts: none -> 5.08 us  [local(): gate_cols, up_cols = (gate_up[:, :, 0], gate_up[:, :, 1])]
  transfers between devices with their start and end apart: 5 -> 7, of which waited for: 1 -> 2; matrix products, arithmetic and copies ran while one was open for 10% -> 14% of each run, Pallas kernels for 47% -> 33%
where the time goes in v3:
time: 243 us; the launch traced here: 242 us
  Pallas kernels  138 us (57%)
  waiting for transfers between devices  26.6 us (11%)
  local copies, waits for them, and re-layouts  24.3 us (10%)
  starting transfers between devices  15.9 us (7%)
  matrix products  14.1 us (6%)
  between operations  13.9 us (6%)
  other arithmetic  8.38 us (3%)
    pallas_call x5, Pallas kernels, exchange(): pl.pallas_call(functools.partial(exchange_kernel, axis, count, gather, re...  69.7 us
    pallas_call x1, Pallas kernels, torus_gather(): pl.pallas_call(functools.partial(torus_gather_kernel, axis, side), out_sh...  25.4 us
    pallas_call x1, Pallas kernels, attention(): pl.pallas_call(functools.partial(attention_kernel, page_len), out_shape=j...  22.6 us
    pallas_call x1, Pallas kernels, torus_sum(): pl.pallas_call(functools.partial(torus_sum_kernel, axis, side), out_shape...  20.6 us
    all_gather x1, waiting for transfers between devices, local(): weights = lax.all_gather(weights, 'dp', axis=1, tiled=True)  19.7 us
    all_to_all x3, starting transfers between devices, spread_weights(): lax.all_to_all(values, 'dp', split_axis=0, concat_axis=0, tiled=True, axi...  14.1 us
    all_to_all x3, waiting for transfers between devices, spread_weights(): lax.all_to_all(values, 'dp', split_axis=0, concat_axis=0, tiled=True, axi...  6.94 us
    dot_general x3, matrix products, dot_t(): lax.dot_general(left, right, (((1,), (1,)), ((), ())), preferred_element_...  5.11 us
  transfers between devices with their start and end apart: 7, of which 2 were waited for; matrix products, arithmetic and copies ran while one was open for 14% of the time, Pallas kernels for 33%

profile of v3, /device:TPU:1, one launch (start us, length us, event | category | flops | bytes accessed | tf_op | source)
XLA Modules:
  0.0 241.5 jit_solution(9952219770352196348)
XLA Ops:
  6.5 1.6 pad_maximum_fusion.1
  8.2 16.1 %row_tokens.1 = bf16[16,8,2304]{2,1,0:T(8,128)(2,1)} custom-call(bf16[8,2304]{1,0:T(8,128)(2,1)} %src_ref.1), custom_call_target="tpu_custom_call" | custom-call | bytes 200000000 | tf_op jit(solution)/shard_map/row_tokens/pallas_call | solution.py:187
  24.2 5.1 %fusion.31 = (bf16[8,144,1,360]{3,2,1,0:T(2,128)(2,1)S(1)}, bf16[8,144,1,360]{3,2,1,0:T(2,128)(2,1)S(1)}) fusion(bf16[8,144,2,360]{3,2,1,0:T(2,128)(2,1)} %param.22), kind=kLoop, calls=%fused_computation.126 | loop fusion | bytes 3317760 | tf_op jit(solution)/shard_map/slice | solution.py:462
  29.4 1.6 copy_bitcast_fusion
  33.7 19.7 %all-gather.2.cloned.1.call-done = bf16[4,2304,128]{2,1,0:T(8,128)(2,1)} async-done(((bf16[4,144,128]{2,1,0:T(8,128)(2,1)}), bf16[4,2304,128]{2,1,0:T(8,128)(2,1)}) %all-gather.2.cloned.1.call-update) | async-done | bytes 2359312 | tf_op jit(solution)/shard_map/all_gather | solution.py:460
  53.4 3.9 %all-to-all-start = ((bf16[8,144,360]{2,1,0:T(8,128)(2,1)}), bf16[8,144,360]{2,1,0:T(8,128)(2,1)S(1)}, u32[]{:S(2)}, u32[]{:S(2)}) async-start(bf16[8,144,360]{2,1,0:T(8,128)(2,1)} %param.23), calls=%async_computation | async-start | bytes 1769472 | tf_op jit(solution)/shard_map/all_to_all | solution.py:451
  57.4 1.0 fusion.7
  58.4 1.1 select_add_fusion.limit_ref
  59.4 2.9 %slice.144.weight_ref = bf16[3,2304,128]{2,1,0:T(8,128)(2,1)} slice(bf16[4,2304,128]{2,1,0:T(8,128)(2,1)} %all-gather.2.cloned.1.call-done), slice={[0:3], [0:2304], [0:128]} | slice | bytes 3538944 | tf_op jit(solution)/shard_map/slice | solution.py:461
  62.3 22.6 %attention.1 = bf16[128,128]{1,0:T(8,128)(2,1)} custom-call(bf16[128,2304]{1,0:T(8,128)(2,1)} %bitcast.117, bf16[1,2304]{1,0:T(2,128)(2,1)} %broadcast_in_dim.126.norm_ref, bf16[3,2304,128]{2,1,0:T(8,128)(2,1)} %slice.144.weight_ref, f32[128,128]{1,0:T(8,128)} %get-tuple-element.58.cos_ref, f32[128,128]{1,0:T(8,128)} %get-tuple-element.57.sin_ref, ...), custom_call_target="tpu_custom_call" | custom-call | flops 1107296256 | bytes 60000000 | tf_op jit(solution)/shard_map/attention/pallas_call | solution.py:106
  86.5 12.8 %leaving.1 = bf16[16,1,2432]{2,1,0:T(2,128)(2,1)} custom-call(bf16[16,1,2432]{2,1,0:T(2,128)(2,1)} %copy.95.src_ref), custom_call_target="tpu_custom_call" | custom-call | bytes 200000000 | tf_op jit(solution)/shard_map/leaving/pallas_call | solution.py:187
  99.3 0.9 copy.138
  100.2 5.8 %all-to-all-start.1 = ((bf16[8,144,360]{2,1,0:T(8,128)(2,1)}), bf16[8,144,360]{2,1,0:T(8,128)(2,1)S(1)}, u32[]{:S(2)}, u32[]{:S(2)}) async-start(bf16[8,144,360]{2,1,0:T(8,128)(2,1)} %get-tuple-element.22), calls=%async_computation.1 | async-start | bytes 1769472 | tf_op jit(solution)/shard_map/all_to_all | solution.py:451
  106.2 2.2 fusion.src_ref
  108.4 15.3 %partial_out.1 = f32[8,2304]{1,0:T(8,128)} custom-call(bf16[16,8,2304]{2,1,0:T(8,128)(2,1)} %fusion.src_ref), custom_call_target="tpu_custom_call" | custom-call | bytes 200000000 | tf_op jit(solution)/shard_map/partial_out/pallas_call | solution.py:187
  123.7 1.0 multiply_reduce_fusion
  124.8 6.9 %all-to-all-done.1 = bf16[8,144,360]{2,1,0:T(8,128)(2,1)S(1)} async-done(((bf16[8,144,360]{2,1,0:T(8,128)(2,1)}), bf16[8,144,360]{2,1,0:T(8,128)(2,1)S(1)}, u32[]{:S(2)}, u32[]{:S(2)}) %all-to-all-start.1) | async-done | bytes 829472 | tf_op jit(solution)/shard_map/all_to_all | solution.py:451
  132.4 1.1 slice_reduce_fusion
  135.4 11.4 %dispatch.1 = bf16[16,2,2304]{2,1,0:T(2,128)(2,1)} custom-call(bf16[16,2,2304]{2,1,0:T(2,128)(2,1)} %bitcast.119), custom_call_target="tpu_custom_call" | custom-call | bytes 200000000 | tf_op jit(solution)/shard_map/dispatch/pallas_call | solution.py:187
  146.8 4.4 %all-to-all-start.2 = ((bf16[8,144,360]{2,1,0:T(8,128)(2,1)}), bf16[8,144,360]{2,1,0:T(8,128)(2,1)}, u32[]{:S(2)}, u32[]{:S(2)}) async-start(bf16[8,144,360]{2,1,0:T(8,128)(2,1)} %get-tuple-element.27), calls=%async_computation.2 | async-start | bytes 1769472 | tf_op jit(solution)/shard_map/all_to_all | solution.py:451
  151.4 1.5 copy.107
  154.0 25.4 %expert_tokens.1 = bf16[4,4,32,2304]{3,2,1,0:T(8,128)(2,1)} custom-call(bf16[32,2304]{1,0:T(8,128)(2,1)} %reshape.266.src_ref), custom_call_target="tpu_custom_call" | custom-call | bytes 60000000 | tf_op jit(solution)/shard_map/expert_tokens/pallas_call | solution.py:283
  179.5 1.5 copy.105
  181.0 1.4 collective-permute-start
  183.0 3.2 %fusion.5 = f32[512,360]{0,1:T(8,128)} fusion(bf16[1152,360]{1,0:T(8,128)(2,1)} %bitcast.115, bf16[512,2304]{1,0:T(8,128)(2,1)} %bitcast.109), kind=kOutput, calls=%fused_computation.16 | convolution fusion | flops 424673280 | bytes 2801664 | tf_op jit(solution)/shard_map/dot_general | solution.py:555
  186.2 2.2 copy.106
  188.5 2.0 convolution_add_fusion.1
  190.6 1.9 fusion.3
  194.2 2.0 convolution_convert_fusion.5
  196.3 20.6 %expert_sums.1 = bf16[32,2304]{1,0:T(8,128)(2,1)S(1)} custom-call(bf16[4,4,32,2304]{3,2,1,0:T(8,128)(2,1)S(1)} %bitcast.106), custom_call_target="tpu_custom_call" | custom-call | tf_op jit(solution)/shard_map/expert_sums/pallas_call | solution.py:395
  217.6 14.2 %back_rows.1 = bf16[16,2,2304]{2,1,0:T(2,128)(2,1)} custom-call(bf16[16,2,2304]{2,1,0:T(2,128)(2,1)} %reshape.271.src_ref), custom_call_target="tpu_custom_call" | custom-call | bytes 200000000 | tf_op jit(solution)/shard_map/back_rows/pallas_call | solution.py:187
  231.9 1.0 fusion.32
  (104 shorter events, 13.5 us)
Async XLA Ops:
  6.5 175.9 %copy-start = (bf16[2304,8]{0,1:T(8,128)(2,1)S(1)}, bf16[2304,8]{0,1:T(8,128)(2,1)}, u32[]{:S(2)}) copy-start(bf16[2304,8]{0,1:T(8,128)(2,1)} %param.21) | copy-start | bytes 110596
  6.5 46.9 %all-gather.2.cloned.1.call-start = ((), (), s32[]{:S(2)}) async-start(), calls=%async_computation.3 | async-start | bytes 2506752 | tf_op jit(solution)/shard_map/all_gather | solution.py:460
  29.3 1.6 copy-start.7
  29.3 3.0 %copy-start.8 = (bf16[2304]{0:T(1024)(128)(2,1)S(1)}, bf16[2304]{0:T(1024)(128)(2,1)}, u32[]{:S(2)}) copy-start(bf16[2304]{0:T(1024)(128)(2,1)} %param.20) | copy-start | bytes 13828
  29.3 3.0 %copy-start.6 = (s32[8,2]{0,1:T(2,128)S(1)}, s32[8,2]{0,1:T(2,128)}, u32[]{:S(2)}) copy-start(s32[8,2]{0,1:T(2,128)} %param.29) | copy-start | bytes 196
  29.4 3.1 %copy-start.5 = (s32[16,8]{0,1:T(8,128)S(1)}, s32[16,8]{0,1:T(8,128)}, u32[]{:S(2)}) copy-start(s32[16,8]{0,1:T(8,128)} %param.28) | copy-start | bytes 1540
  29.4 4.1 %copy-start.11 = (s32[128]{0:T(128)S(1)}, s32[128]{0:T(128)}, u32[]{:S(2)}) copy-start(s32[128]{0:T(128)} %param.27) | copy-start | bytes 1540
  29.4 4.1 %copy-start.9 = (s32[4,4]{1,0:T(4,128)S(1)}, s32[4,4]{1,0:T(4,128)}, u32[]{:S(2)}) copy-start(s32[4,4]{1,0:T(4,128)} %param.25) | copy-start | bytes 196
  31.0 26.4 %copy-start.10 = (s32[128,4]{0,1:T(4,128)S(1)}, s32[128,4]{0,1:T(4,128)}, u32[]{:S(2)}) copy-start(s32[128,4]{0,1:T(4,128)} %param.26) | copy-start | bytes 6148
  53.4 32.4 %all-to-all-start = ((bf16[8,144,360]{2,1,0:T(8,128)(2,1)}), bf16[8,144,360]{2,1,0:T(8,128)(2,1)S(1)}, u32[]{:S(2)}, u32[]{:S(2)}) async-start(bf16[8,144,360]{2,1,0:T(8,128)(2,1)} %param.23), calls=%async_computation | async-start | bytes 1769472 | tf_op jit(solution)/shard_map/all_to_all | solution.py:451
  84.9 21.2 %slice-start = ((bf16[128,128]{1,0:T(8,128)(2,1)}), bf16[120,128]{1,0:T(8,128)(2,1)S(1)}, s32[]{:S(2)}) async-start(bf16[128,128]{1,0:T(8,128)(2,1)} %attention.1), calls=%async_computation.4 | async-start | bytes 61440 | tf_op jit(solution)/shard_map/slice | solution.py:496
  100.2 23.4 %copy-start.4 = (bf16[8,2304]{1,0:T(8,128)(2,1)S(1)}, bf16[8,2304]{1,0:T(8,128)(2,1)}, u32[]{:S(2)}) copy-start(bf16[8,2304]{1,0:T(8,128)(2,1)} %src_ref.1) | copy-start | bytes 110596
  100.2 31.5 %all-to-all-start.1 = ((bf16[8,144,360]{2,1,0:T(8,128)(2,1)}), bf16[8,144,360]{2,1,0:T(8,128)(2,1)S(1)}, u32[]{:S(2)}, u32[]{:S(2)}) async-start(bf16[8,144,360]{2,1,0:T(8,128)(2,1)} %get-tuple-element.22), calls=%async_computation.1 | async-start | bytes 1769472 | tf_op jit(solution)/shard_map/all_to_all | solution.py:451
  131.7 47.7 %copy-start.2 = (bf16[8,144,360]{2,1,0:T(8,128)(2,1)}, bf16[8,144,360]{2,1,0:T(8,128)(2,1)S(1)}, u32[]{:S(2)}) copy-start(bf16[8,144,360]{2,1,0:T(8,128)(2,1)S(1)} %all-to-all-done.1) | copy-start | bytes 2488324
  146.8 6.5 %copy-start.3 = (bf16[16,2,2304]{2,1,0:T(2,128)(2,1)S(1)}, bf16[16,2,2304]{2,1,0:T(2,128)(2,1)}, u32[]{:S(2)}) copy-start(bf16[16,2,2304]{2,1,0:T(2,128)(2,1)} %dispatch.1) | copy-start | bytes 442372
  146.8 39.4 %all-to-all-start.2 = ((bf16[8,144,360]{2,1,0:T(8,128)(2,1)}), bf16[8,144,360]{2,1,0:T(8,128)(2,1)}, u32[]{:S(2)}, u32[]{:S(2)}) async-start(bf16[8,144,360]{2,1,0:T(8,128)(2,1)} %get-tuple-element.27), calls=%async_computation.2 | async-start | bytes 1769472 | tf_op jit(solution)/shard_map/all_to_all | solution.py:451
  152.9 41.2 %collective-permute-start.2 = (bf16[1152,360]{0,1:T(8,128)(2,1)}, bf16[1152,360]{0,1:T(8,128)(2,1)}, u32[]{:S(2)}, u32[]{:S(2)}) collective-permute-start(bf16[1152,360]{0,1:T(8,128)(2,1)} %copy.107), channel_id=1, source_target_pairs={{0,16},{16,0},{32,48},{48,32},{64,80},{80,64},{96,112},{112,96},{1... | collective-permute-start | bytes 2488328 | tf_op jit(solution)/shard_map/ppermute | solution.py:490
  181.0 7.6 %collective-permute-start = (bf16[1152,360]{0,1:T(8,128)(2,1)}, bf16[1152,360]{0,1:T(8,128)(2,1)}, u32[]{:S(2)}, u32[]{:S(2)}) collective-permute-start(bf16[1152,360]{0,1:T(8,128)(2,1)} %copy.105), channel_id=1, source_target_pairs={{0,16},{16,0},{32,48},{48,32},{64,80},{80,64},{96,112},{112,96},{1... | collective-permute-start | bytes 2488328 | tf_op jit(solution)/shard_map/ppermute | solution.py:548
  183.0 5.6 %copy-start.1 = (bf16[4,4,32,2304]{3,2,1,0:T(8,128)(2,1)S(1)}, bf16[4,4,32,2304]{3,2,1,0:T(8,128)(2,1)}, u32[]{:S(2)}) copy-start(bf16[4,4,32,2304]{3,2,1,0:T(8,128)(2,1)} %expert_tokens.1) | copy-start | bytes 7077892
  188.5 4.0 %collective-permute-start.1 = (bf16[1152,360]{0,1:T(8,128)(2,1)}, bf16[1152,360]{0,1:T(8,128)(2,1)S(1)}, u32[]{:S(2)}, u32[]{:S(2)}) collective-permute-start(bf16[1152,360]{0,1:T(8,128)(2,1)} %copy.106), channel_id=1, source_target_pairs={{0,16},{16,0},{32,48},{48,32},{64,80},{80,64},{96,112},{112,96},{1... | collective-permute-start | bytes 2488328 | tf_op jit(solution)/shard_map/ppermute | solution.py:550
Sparse Core Ops, SparseCore 0:
  9.2 44.1 all-gather.1

commit v4 on v3

--- a/solution.py
+++ b/solution.py
@@ -194,6 +194,106 @@
         cost_estimate=pl.CostEstimate(flops=0, bytes_accessed=200_000_000, transcendentals=0),
         name=name,
     )(values)
+
+
+def prologue_kernel(
+    ring, count, token_ref, weight_ref, tokens_out, weights_out,
+    token_send, token_recv, right_send, right_recv, left_send, left_recv,
+    pair_send, pair_recv, own_sem,
+):
+    me = lax.axis_index("fsdp")
+    row = lax.axis_index("dp")
+    chip, core = row // 2, lax.rem(row, 2)
+
+    def place(step):
+        return lax.rem(chip + step, ring) * 2 + core
+
+    partner = {"dp": chip * 2 + (1 - core)}
+    after = {"dp": place(1)}
+    before = {"dp": place(ring - 1)}
+    peers = [{"fsdp": lax.rem(me + step, count)} for step in range(1, count)]
+    barrier = pltpu.get_barrier_semaphore()
+    for device in peers + [partner, after, before]:
+        pl.semaphore_signal(
+            barrier, inc=1, device_id=device, device_id_type=pl.DeviceIdType.MESH
+        )
+    pl.semaphore_wait(barrier, count + 2)
+
+    def send(src, dst, send_sem, recv_sem, device):
+        copy = pltpu.make_async_remote_copy(
+            src_ref=src,
+            dst_ref=dst,
+            send_sem=send_sem,
+            recv_sem=recv_sem,
+            device_id=device,
+            device_id_type=pl.DeviceIdType.MESH,
+        )
+        copy.start()
+        return copy
+
+    def slot(step):
+        return weights_out.at[:, place(step)]
+
+    rights = ring // 2
+    lefts = ring - 1 - rights
+    right = send(weight_ref, slot(0), right_send.at[0], right_recv.at[0], after)
+    left = send(weight_ref, slot(0), left_send.at[0], left_recv.at[0], before)
+    tail = [send(weight_ref, slot(0), pair_send.at[0], pair_recv.at[0], partner)]
+    for step, device in enumerate(peers):
+        tail.append(
+            send(token_ref, tokens_out.at[me], token_send.at[step], token_recv.at[step], device)
+        )
+    own = [
+        pltpu.make_async_copy(weight_ref, slot(0), own_sem.at[0]),
+        pltpu.make_async_copy(token_ref, tokens_out.at[me], own_sem.at[1]),
+    ]
+    for copy in own:
+        copy.start()
+    for s in range(1, rights + 1):
+        right.wait()
+        block = slot(ring - s)
+        if s < rights:
+            right = send(block, block, right_send.at[s], right_recv.at[s], after)
+        tail.append(send(block, block, pair_send.at[s], pair_recv.at[s], partner))
+        if s <= lefts:
+            left.wait()
+            block = slot(s)
+            if s < lefts:
+                left = send(block, block, left_send.at[s], left_recv.at[s], before)
+            tail.append(
+                send(block, block, pair_send.at[rights + s], pair_recv.at[rights + s], partner)
+            )
+    for copy in own + tail:
+        copy.wait()
+
+
+def prologue(tokens, weights, number):
+    rows_count = lax.axis_size("dp")
+    count = lax.axis_size("fsdp")
+    ring = rows_count // 2
+    parts, depth, width = weights.shape
+    return pl.pallas_call(
+        functools.partial(prologue_kernel, ring, count),
+        out_shape=(
+            jax.ShapeDtypeStruct((count,) + tokens.shape, tokens.dtype),
+            jax.ShapeDtypeStruct((parts, rows_count, depth, width), weights.dtype),
+        ),
+        in_specs=[vmem()] * 2,
+        out_specs=(vmem(), vmem()),
+        scratch_shapes=[
+            pltpu.SemaphoreType.DMA((count - 1,)),
+            pltpu.SemaphoreType.DMA((count - 1,)),
+            pltpu.SemaphoreType.DMA((ring,)),
+            pltpu.SemaphoreType.DMA((ring,)),
+            pltpu.SemaphoreType.DMA((ring,)),
+            pltpu.SemaphoreType.DMA((ring,)),
+            pltpu.SemaphoreType.DMA((ring,)),
+            pltpu.SemaphoreType.DMA((ring,)),
+            pltpu.SemaphoreType.DMA((2,)),
+        ],
+        compiler_params=pltpu.CompilerParams(collective_id=number, has_side_effects=True),
+        name="prologue",
+    )(tokens, weights)
 
 
 def torus_ids(axis, side):
@@ -452,16 +552,15 @@
             values, "dp", split_axis=0, concat_axis=0, tiled=True, axis_index_groups=same_core
         )
 
-    row_tokens = exchange(hidden_in, "fsdp", 0, "row_tokens", gather=True)
-    row_tokens = row_tokens.reshape(req_row, model_width)
     weights = jnp.concatenate(
         [jnp.transpose(project_in, (1, 0, 2)), project_out.T[None]], axis=0
     )
-    weights = lax.all_gather(weights, "dp", axis=1, tiled=True)
-    weight_in, weight_out = weights[:3], weights[3]
-    gate_cols, up_cols = gate_up[:, :, 0], gate_up[:, :, 1]
-    row_tokens, gate_cols, up_cols = lax.optimization_barrier((row_tokens, gate_cols, up_cols))
-    expert_down, weights = lax.optimization_barrier((expert_down, weights))
+    row_tokens, weights = prologue(hidden_in, weights, 0)
+    row_tokens = row_tokens.reshape(req_row, model_width)
+    weights = weights.reshape(weights.shape[0], model_width, head_cols)
+    weight_out = weights[3]
+    gate_cols = gate_up[:, :, 0]
+    expert_down, weights, gate_cols = lax.optimization_barrier((expert_down, weights, gate_cols))
     swap = [(d, d ^ 1) for d in range(rows_count)]
     down_own = spread_weights(expert_down)
 
@@ -477,7 +576,7 @@
         valid = jnp.clip(position - page_len * j, 0, page_len)
         limit += jnp.where(page_list[:, j : j + 1] == page_numbers[None, :], valid[:, None], 0)
 
-    heads_out = attention(row_tokens, norm_first, weight_in, position, limit, cache_pool)
+    heads_out = attention(row_tokens, norm_first, weights, position, limit, cache_pool)
 
     row_numbers = jnp.arange(rows_count, dtype=jnp.int32)
     send_select = (move_target[my_row][None, :] == row_numbers[:, None]).astype(BF16)
@@ -505,9 +604,11 @@
         "partial_out",
         reduce=F32,
     )
+    attn_proj, gate_up = lax.optimization_barrier((attn_proj, gate_up))
+    up_cols = gate_up[:, :, 1]
     resid = mine_tokens.astype(F32) + attn_proj
     moe_in = rms_scale(resid, norm_second).astype(BF16)
-    moe_in, gate_own = lax.optimization_barrier((moe_in, gate_own))
+    moe_in, gate_own, up_cols = lax.optimization_barrier((moe_in, gate_own, up_cols))
     logits = jnp.dot(moe_in, router, preferred_element_type=F32)
     expert_ids = jnp.arange(expert_count, dtype=jnp.int32)
     picked = routes[:, :, None] == expert_ids[None, None, :]

time: 243 us -> 219 us (0.901)
  waiting for transfers between devices: 26.6 us -> 10.2 us
  between operations: 13.9 us -> 0.5 us
  Pallas kernels: 138 us -> 151 us
  local copies, waits for them, and re-layouts: 24.3 us -> 21.2 us
    pallas_call x0 -> x1, Pallas kernels: none -> 35.1 us  [prologue(): pl.pallas_call(functools.partial(prologue_kernel, ring, count), out_shape...]
    all_gather x1 -> x0, waiting for transfers between devices: 19.7 us -> none  [local(): weights = lax.all_gather(weights, 'dp', axis=1, tiled=True)]
    pallas_call x5 -> x4, Pallas kernels: 69.7 us -> 50.3 us  [exchange(): pl.pallas_call(functools.partial(exchange_kernel, axis, count, gather, re...]
    slice x2 -> x1, local copies, waits for them, and re-layouts: 7.93 us -> 1.1 us  [local(): weight_out = weights[3]]
    all_to_all x3, waiting for transfers between devices: 6.94 us -> 10.2 us  [spread_weights(): lax.all_to_all(values, 'dp', split_axis=0, concat_axis=0, tiled=True, axi...]
    unnamed x29 -> x36, local copies, waits for them, and re-layouts: 1.15 us -> 4.34 us
    pallas_call x1, Pallas kernels: 25.4 us -> 22.9 us  [torus_gather(): pl.pallas_call(functools.partial(torus_gather_kernel, axis, side), out_sh...]
  transfers between devices with their start and end apart: 7 -> 6, of which waited for: 2 -> 1; matrix products, arithmetic and copies ran while one was open for 14% -> 12% of each run, Pallas kernels for 33% -> 27%
where the time goes in v4:
time: 219 us; the launch traced here: 218 us
  Pallas kernels  151 us (69%)
  local copies, waits for them, and re-layouts  21.2 us (10%)
  starting transfers between devices  15.5 us (7%)
  matrix products  13.1 us (6%)
  waiting for transfers between devices  10.2 us (5%)
  other arithmetic  6.51 us (3%)
    pallas_call x4, Pallas kernels, exchange(): pl.pallas_call(functools.partial(exchange_kernel, axis, count, gather, re...  50.3 us
    pallas_call x1, Pallas kernels, prologue(): pl.pallas_call(functools.partial(prologue_kernel, ring, count), out_shape...  35.1 us
    pallas_call x1, Pallas kernels, torus_gather(): pl.pallas_call(functools.partial(torus_gather_kernel, axis, side), out_sh...  22.9 us
    pallas_call x1, Pallas kernels, attention(): pl.pallas_call(functools.partial(attention_kernel, page_len), out_shape=j...  22.8 us
    pallas_call x1, Pallas kernels, torus_sum(): pl.pallas_call(functools.partial(torus_sum_kernel, axis, side), out_shape...  20.3 us
    all_to_all x3, starting transfers between devices, spread_weights(): lax.all_to_all(values, 'dp', split_axis=0, concat_axis=0, tiled=True, axi...  13.7 us
    all_to_all x3, waiting for transfers between devices, spread_weights(): lax.all_to_all(values, 'dp', split_axis=0, concat_axis=0, tiled=True, axi...  10.2 us
  transfers between devices with their start and end apart: 6, of which 1 were waited for; matrix products, arithmetic and copies ran while one was open for 12% of the time, Pallas kernels for 27%

profile of v4, /device:TPU:1, one launch (start us, length us, event | category | flops | bytes accessed | tf_op | source)
XLA Modules:
  0.0 218.4 jit_solution(7495349918206960871)
XLA Ops:
  0.0 2.6 %copy.136 = bf16[8,144,1,360]{3,1,0,2:T(8,128)(2,1)} copy(bf16[8,144,1,360]{3,2,1,0:T(2,128)(2,1)} %bitcast.113) | data formatting | bytes 1658880
  3.3 35.1 %prologue.1 = (bf16[16,8,2304]{2,1,0:T(8,128)(2,1)}, bf16[4,16,144,128]{3,2,1,0:T(8,128)(2,1)}) custom-call(bf16[8,2304]{1,0:T(8,128)(2,1)} %token_ref.1, bf16[4,144,128]{2,1,0:T(8,128)(2,1)} %pad_maximum_fusion.1.weight_ref), custom_call_target="tpu_custom_call" | custom-call | tf_op jit(solution)/shard_map/prologue/pallas_call | solution.py:275
  38.4 3.6 %all-to-all-start = ((bf16[8,144,360]{2,1,0:T(8,128)(2,1)}), bf16[8,144,360]{2,1,0:T(8,128)(2,1)S(1)}, u32[]{:S(2)}, u32[]{:S(2)}) async-start(bf16[8,144,360]{2,1,0:T(8,128)(2,1)} %param.23), calls=%async_computation | async-start | bytes 1769472 | tf_op jit(solution)/shard_map/all_to_all | solution.py:551
  42.0 1.1 slice.125
  44.6 0.9 fusion.7
  45.6 1.1 select_add_fusion.limit_ref
  46.6 22.8 %attention.1 = bf16[128,128]{1,0:T(8,128)(2,1)} custom-call(bf16[128,2304]{1,0:T(8,128)(2,1)} %bitcast.122, bf16[1,2304]{1,0:T(2,128)(2,1)} %broadcast_in_dim.127.norm_ref, bf16[4,2304,128]{2,1,0:T(8,128)(2,1)} %bitcast.119, f32[128,128]{1,0:T(8,128)} %get-tuple-element.64.cos_ref, f32[128,128]{1,0:T(8,128)} %get-tuple-element.63.sin_ref, ...), custom_call_target="tpu_custom_call" | custom-call | flops 1107296256 | bytes 60000000 | tf_op jit(solution)/shard_map/attention/pallas_call | solution.py:106
  70.7 0.9 slice_bitcast_fusion.1
  72.5 12.3 %leaving.1 = bf16[16,1,2432]{2,1,0:T(2,128)(2,1)} custom-call(bf16[16,1,2432]{2,1,0:T(2,128)(2,1)} %copy.94.src_ref), custom_call_target="tpu_custom_call" | custom-call | bytes 200000000 | tf_op jit(solution)/shard_map/leaving/pallas_call | solution.py:187
  84.8 0.9 copy.137
  85.9 5.8 %all-to-all-start.1 = ((bf16[8,144,360]{2,1,0:T(8,128)(2,1)}), bf16[8,144,360]{2,1,0:T(8,128)(2,1)}, u32[]{:S(2)}, u32[]{:S(2)}) async-start(bf16[8,144,360]{2,1,0:T(8,128)(2,1)} %bitcast.120), calls=%async_computation.1 | async-start | bytes 1769472 | tf_op jit(solution)/shard_map/all_to_all | solution.py:551
  91.6 1.1 fusion.src_ref
  92.8 12.3 %partial_out.1 = f32[8,2304]{1,0:T(8,128)} custom-call(bf16[16,8,2304]{2,1,0:T(8,128)(2,1)} %fusion.src_ref), custom_call_target="tpu_custom_call" | custom-call | bytes 200000000 | tf_op jit(solution)/shard_map/partial_out/pallas_call | solution.py:187
  106.1 1.0 slice_bitcast_fusion
  107.2 10.2 %all-to-all-done.1 = bf16[8,144,360]{2,1,0:T(8,128)(2,1)} async-done(((bf16[8,144,360]{2,1,0:T(8,128)(2,1)}), bf16[8,144,360]{2,1,0:T(8,128)(2,1)}, u32[]{:S(2)}, u32[]{:S(2)}) %all-to-all-start.1) | async-done | bytes 829472 | tf_op jit(solution)/shard_map/all_to_all | solution.py:551
  118.1 1.1 slice_reduce_fusion
  120.2 0.9 pad_maximum_fusion.2
  121.1 11.4 %dispatch.1 = bf16[16,2,2304]{2,1,0:T(2,128)(2,1)} custom-call(bf16[16,2,2304]{2,1,0:T(2,128)(2,1)} %bitcast.124), custom_call_target="tpu_custom_call" | custom-call | bytes 200000000 | tf_op jit(solution)/shard_map/dispatch/pallas_call | solution.py:187
  132.5 4.4 %all-to-all-start.2 = ((bf16[8,144,360]{2,1,0:T(8,128)(2,1)}), bf16[8,144,360]{2,1,0:T(8,128)(2,1)}, u32[]{:S(2)}, u32[]{:S(2)}) async-start(bf16[8,144,360]{2,1,0:T(8,128)(2,1)} %slice_bitcast_fusion), calls=%async_computation.2 | async-start | bytes 1769472 | tf_op jit(solution)/shard_map/all_to_all | solution.py:551
  137.1 1.5 copy.107
  139.7 22.9 %expert_tokens.1 = bf16[4,4,32,2304]{3,2,1,0:T(8,128)(2,1)} custom-call(bf16[32,2304]{1,0:T(8,128)(2,1)} %reshape.273.src_ref), custom_call_target="tpu_custom_call" | custom-call | bytes 60000000 | tf_op jit(solution)/shard_map/expert_tokens/pallas_call | solution.py:383
  162.6 2.3 %copy.105 = bf16[1152,360]{0,1:T(8,128)(2,1)} copy(bf16[1152,360]{1,0:T(8,128)(2,1)} %bitcast.36) | data formatting | bytes 1658880 | tf_op jit(solution)/shard_map/reshape | solution.py:646
  164.9 1.4 collective-permute-start
  166.9 3.3 %fusion.5 = f32[512,360]{0,1:T(8,128)} fusion(bf16[1152,360]{1,0:T(8,128)(2,1)} %bitcast.36, bf16[512,2304]{1,0:T(8,128)(2,1)} %bitcast.114), kind=kOutput, calls=%fused_computation.16 | convolution fusion | flops 424673280 | bytes 2801664 | tf_op jit(solution)/shard_map/dot_general | solution.py:656
  170.2 2.2 %copy.106 = bf16[1152,360]{0,1:T(8,128)(2,1)} copy(bf16[1152,360]{1,0:T(8,128)(2,1)} %bitcast.37) | data formatting | bytes 1658880 | tf_op jit(solution)/shard_map/reshape | solution.py:650
  172.5 2.1 convolution_add_fusion.1
  174.5 1.9 fusion.3
  177.2 0.9 convolution_convert_fusion.4
  178.1 2.0 convolution_convert_fusion.5
  180.3 20.3 %expert_sums.1 = bf16[32,2304]{1,0:T(8,128)(2,1)S(1)} custom-call(bf16[4,4,32,2304]{3,2,1,0:T(8,128)(2,1)S(1)} %bitcast.110), custom_call_target="tpu_custom_call" | custom-call | tf_op jit(solution)/shard_map/expert_sums/pallas_call | solution.py:495
  201.3 14.3 %back_rows.1 = bf16[16,2,2304]{2,1,0:T(2,128)(2,1)} custom-call(bf16[16,2,2304]{2,1,0:T(2,128)(2,1)} %reshape.278.src_ref), custom_call_target="tpu_custom_call" | custom-call | bytes 200000000 | tf_op jit(solution)/shard_map/back_rows/pallas_call | solution.py:187
  215.6 1.0 fusion.31
  (108 shorter events, 12.6 us)
Async XLA Ops:
  0.0 166.3 %copy-start = (bf16[2304,8]{0,1:T(8,128)(2,1)S(1)}, bf16[2304,8]{0,1:T(8,128)(2,1)}, u32[]{:S(2)}) copy-start(bf16[2304,8]{0,1:T(8,128)(2,1)} %param.21) | copy-start | bytes 110596
  0.0 2.6 %copy-start.7 = (bf16[128,144]{0,1:T(8,128)(2,1)S(1)}, bf16[128,144]{0,1:T(8,128)(2,1)}, u32[]{:S(2)}) copy-start(bf16[128,144]{0,1:T(8,128)(2,1)} %param.18) | copy-start | bytes 110596
  0.0 2.6 %copy-start.6 = (bf16[144,3,128]{2,0,1:T(8,128)(2,1)S(1)}, bf16[144,3,128]{2,0,1:T(8,128)(2,1)}, u32[]{:S(2)}) copy-start(bf16[144,3,128]{2,0,1:T(8,128)(2,1)} %param.17) | copy-start | bytes 331780
  2.6 40.5 %copy-start.10 = (bf16[2304]{0:T(1024)(128)(2,1)S(1)}, bf16[2304]{0:T(1024)(128)(2,1)}, u32[]{:S(2)}) copy-start(bf16[2304]{0:T(1024)(128)(2,1)} %param.19) | copy-start | bytes 13828
  2.6 41.9 %copy-start.14 = (s32[128]{0:T(128)S(1)}, s32[128]{0:T(128)}, u32[]{:S(2)}) copy-start(s32[128]{0:T(128)} %param.27) | copy-start | bytes 1540
  2.6 41.9 %copy-start.12 = (s32[4,4]{1,0:T(4,128)S(1)}, s32[4,4]{1,0:T(4,128)}, u32[]{:S(2)}) copy-start(s32[4,4]{1,0:T(4,128)} %param.25) | copy-start | bytes 196
  2.6 42.0 %copy-start.13 = (s32[128,4]{0,1:T(4,128)S(1)}, s32[128,4]{0,1:T(4,128)}, u32[]{:S(2)}) copy-start(s32[128,4]{0,1:T(4,128)} %param.26) | copy-start | bytes 6148
  38.4 33.3 %all-to-all-start = ((bf16[8,144,360]{2,1,0:T(8,128)(2,1)}), bf16[8,144,360]{2,1,0:T(8,128)(2,1)S(1)}, u32[]{:S(2)}, u32[]{:S(2)}) async-start(bf16[8,144,360]{2,1,0:T(8,128)(2,1)} %param.23), calls=%async_computation | async-start | bytes 1769472 | tf_op jit(solution)/shard_map/all_to_all | solution.py:551
  46.6 23.5 %copy-start.11 = (bf16[2304]{0:T(1024)(128)(2,1)S(1)}, bf16[2304]{0:T(1024)(128)(2,1)}, u32[]{:S(2)}) copy-start(bf16[2304]{0:T(1024)(128)(2,1)} %param.20) | copy-start | bytes 13828
  46.6 23.5 %copy-start.9 = (s32[8,2]{0,1:T(2,128)S(1)}, s32[8,2]{0,1:T(2,128)}, u32[]{:S(2)}) copy-start(s32[8,2]{0,1:T(2,128)} %param.29) | copy-start | bytes 196
  46.6 23.7 %copy-start.8 = (s32[16,8]{0,1:T(8,128)S(1)}, s32[16,8]{0,1:T(8,128)}, u32[]{:S(2)}) copy-start(s32[16,8]{0,1:T(8,128)} %param.28) | copy-start | bytes 1540
  69.4 22.2 %slice-start = ((bf16[128,128]{1,0:T(8,128)(2,1)}), bf16[120,128]{1,0:T(8,128)(2,1)S(1)}, s32[]{:S(2)}) async-start(bf16[128,128]{1,0:T(8,128)(2,1)} %attention.1), calls=%async_computation.3 | async-start | bytes 61440 | tf_op jit(solution)/shard_map/slice | solution.py:595
  70.7 34.4 %copy-start.1 = (bf16[8,144,2,360]{3,2,1,0:T(2,128)(2,1)S(1)}, bf16[8,144,2,360]{3,2,1,0:T(2,128)(2,1)}, u32[]{:S(2)}) copy-start(bf16[8,144,2,360]{3,2,1,0:T(2,128)(2,1)} %param.22) | copy-start | bytes 4976644
  85.9 31.6 %all-to-all-start.1 = ((bf16[8,144,360]{2,1,0:T(8,128)(2,1)}), bf16[8,144,360]{2,1,0:T(8,128)(2,1)}, u32[]{:S(2)}, u32[]{:S(2)}) async-start(bf16[8,144,360]{2,1,0:T(8,128)(2,1)} %bitcast.120), calls=%async_computation.1 | async-start | bytes 1769472 | tf_op jit(solution)/shard_map/all_to_all | solution.py:551
  92.8 12.5 %copy-start.5 = (bf16[8,2304]{1,0:T(8,128)(2,1)S(1)}, bf16[8,2304]{1,0:T(8,128)(2,1)}, u32[]{:S(2)}) copy-start(bf16[8,2304]{1,0:T(8,128)(2,1)} %token_ref.1) | copy-start | bytes 110596
  105.1 0.9 copy-start.4
  132.5 6.5 %copy-start.3 = (bf16[16,2,2304]{2,1,0:T(2,128)(2,1)S(1)}, bf16[16,2,2304]{2,1,0:T(2,128)(2,1)}, u32[]{:S(2)}) copy-start(bf16[16,2,2304]{2,1,0:T(2,128)(2,1)} %dispatch.1) | copy-start | bytes 442372
  132.5 37.7 %all-to-all-start.2 = ((bf16[8,144,360]{2,1,0:T(8,128)(2,1)}), bf16[8,144,360]{2,1,0:T(8,128)(2,1)}, u32[]{:S(2)}, u32[]{:S(2)}) async-start(bf16[8,144,360]{2,1,0:T(8,128)(2,1)} %slice_bitcast_fusion), calls=%async_computation.2 | async-start | bytes 1769472 | tf_op jit(solution)/shard_map/all_to_all | solution.py:551
  138.6 39.5 %collective-permute-start.2 = (bf16[1152,360]{0,1:T(8,128)(2,1)}, bf16[1152,360]{0,1:T(8,128)(2,1)}, u32[]{:S(2)}, u32[]{:S(2)}) collective-permute-start(bf16[1152,360]{0,1:T(8,128)(2,1)} %copy.107), channel_id=1, source_target_pairs={{0,16},{16,0},{32,48},{48,32},{64,80},{80,64},{96,112},{112,96},{1... | collective-permute-start | bytes 2488328 | tf_op jit(solution)/shard_map/ppermute | solution.py:589
  164.9 7.6 %collective-permute-start = (bf16[1152,360]{0,1:T(8,128)(2,1)}, bf16[1152,360]{0,1:T(8,128)(2,1)}, u32[]{:S(2)}, u32[]{:S(2)}) collective-permute-start(bf16[1152,360]{0,1:T(8,128)(2,1)} %copy.105), channel_id=1, source_target_pairs={{0,16},{16,0},{32,48},{48,32},{64,80},{80,64},{96,112},{112,96},{1... | collective-permute-start | bytes 2488328 | tf_op jit(solution)/shard_map/ppermute | solution.py:649
  166.8 5.7 %copy-start.2 = (bf16[4,4,32,2304]{3,2,1,0:T(8,128)(2,1)S(1)}, bf16[4,4,32,2304]{3,2,1,0:T(8,128)(2,1)}, u32[]{:S(2)}) copy-start(bf16[4,4,32,2304]{3,2,1,0:T(8,128)(2,1)} %expert_tokens.1) | copy-start | bytes 7077892
  172.4 4.0 %collective-permute-start.1 = (bf16[1152,360]{0,1:T(8,128)(2,1)}, bf16[1152,360]{0,1:T(8,128)(2,1)S(1)}, u32[]{:S(2)}, u32[]{:S(2)}) collective-permute-start(bf16[1152,360]{0,1:T(8,128)(2,1)} %copy.106), channel_id=1, source_target_pairs={{0,16},{16,0},{32,48},{48,32},{64,80},{80,64},{96,112},{112,96},{1... | collective-permute-start | bytes 2488328 | tf_op jit(solution)/shard_map/ppermute | solution.py:651

commit v5 on v4

--- a/solution.py
+++ b/solution.py
@@ -294,6 +294,52 @@
         compiler_params=pltpu.CompilerParams(collective_id=number, has_side_effects=True),
         name="prologue",
     )(tokens, weights)
+
+
+def hidden_kernel(token_ref, gate_own, gate_other, up_own, gate_ref, up_ref):
+    half = gate_own.shape[0]
+    own = token_ref[:, :half]
+    other = token_ref[:, half:]
+    gate = jnp.dot(own, gate_own[...], preferred_element_type=F32)
+    gate = gate + jnp.dot(other, gate_other[...], preferred_element_type=F32)
+    gate_ref[...] = gate / (1.0 + jnp.exp(-gate))
+    up_ref[...] = jnp.dot(own, up_own[...], preferred_element_type=F32)
+
+
+def down_kernel(token_ref, gate_ref, up_ref, up_other, down_own, down_other, out_ref):
+    half = up_other.shape[0]
+    up = up_ref[...] + jnp.dot(
+        token_ref[:, half:], up_other[...], preferred_element_type=F32
+    )
+    activation = (gate_ref[...] * up).astype(BF16)
+    out_ref[:, :half] = dot_t(activation, down_own[...]).astype(BF16)
+    out_ref[:, half:] = dot_t(activation, down_other[...]).astype(BF16)
+
+
+def experts(tokens, gates, ups, downs):
+    count, width = tokens.shape
+    depth, units = gates[0].shape
+    part = jax.ShapeDtypeStruct((count, units), F32)
+    params = pltpu.CompilerParams(vmem_limit_bytes=40 * 1024 * 1024)
+    gate, up = pl.pallas_call(
+        hidden_kernel,
+        out_shape=(part, part),
+        in_specs=[vmem()] * 4,
+        out_specs=(vmem(), vmem()),
+        compiler_params=params,
+        cost_estimate=pl.CostEstimate(
+            flops=6 * count * depth * units, bytes_accessed=30_000_000, transcendentals=0
+        ),
+        name="experts_hidden",
+    )(tokens, gates[0], gates[1], ups[0])
+    return pl.pallas_call(
+        down_kernel,
+        out_shape=jax.ShapeDtypeStruct((count, width), BF16),
+        in_specs=[vmem()] * 6,
+        out_specs=vmem(),
+        compiler_params=params,
+        name="experts_down",
+    )(tokens, gate, up, ups[1], downs[0], downs[1])
 
 
 def torus_ids(axis, side):
@@ -559,7 +605,13 @@
     row_tokens = row_tokens.reshape(req_row, model_width)
     weights = weights.reshape(weights.shape[0], model_width, head_cols)
     weight_out = weights[3]
-    gate_cols = gate_up[:, :, 0]
+    units_wide = -(-units_here // 128) * 128
+
+    def widen(values):
+        return jnp.pad(values, ((0, 0), (0, 0), (0, units_wide - units_here)))
+
+    gate_cols = widen(gate_up[:, :, 0])
+    expert_down = widen(expert_down)
     expert_down, weights, gate_cols = lax.optimization_barrier((expert_down, weights, gate_cols))
     swap = [(d, d ^ 1) for d in range(rows_count)]
     down_own = spread_weights(expert_down)
@@ -583,7 +635,7 @@
     leaving = jnp.concatenate([heads_out[staying:], row_tokens[staying:]], axis=1)
     leaving_send = jnp.dot(send_select, leaving, preferred_element_type=F32).astype(BF16)
     leaving_send, down_own = lax.optimization_barrier((leaving_send, down_own))
-    down_own = down_own.reshape(-1, units_here)
+    down_own = down_own.reshape(-1, units_wide)
     leaving_recv = exchange(leaving_send[:, None, :], "dp", 1, "leaving")[:, 0]
     leaving_recv, gate_cols = lax.optimization_barrier((leaving_recv, gate_cols))
     down_other = lax.ppermute(down_own, "dp", swap)
@@ -605,7 +657,7 @@
         reduce=F32,
     )
     attn_proj, gate_up = lax.optimization_barrier((attn_proj, gate_up))
-    up_cols = gate_up[:, :, 1]
+    up_cols = widen(gate_up[:, :, 1])
     resid = mine_tokens.astype(F32) + attn_proj
     moe_in = rms_scale(resid, norm_second).astype(BF16)
     moe_in, gate_own, up_cols = lax.optimization_barrier((moe_in, gate_own, up_cols))
@@ -643,26 +695,19 @@
         ],
         axis=1,
     ).reshape(rows_count, slots_row, model_width)
-    gate_own = gate_own.reshape(-1, units_here)
+    gate_own = gate_own.reshape(-1, units_wide)
     received = exchange(dispatch, "dp", 3, "dispatch")
     received, up_cols = lax.optimization_barrier((received, up_cols))
     gate_other = lax.ppermute(gate_own, "dp", swap)
-    up_own = spread_weights(up_cols).reshape(-1, units_here)
-    up_other = lax.ppermute(up_own, "dp", swap)
+    up_own = spread_weights(up_cols).reshape(-1, units_wide)
     expert_tokens = torus_gather(
         received.reshape(rows_count * slots_row, model_width), "fsdp", 4, "expert_tokens"
     )
+    expert_tokens, up_own = lax.optimization_barrier((expert_tokens, up_own))
+    up_other = lax.ppermute(up_own, "dp", swap)
     flattened = expert_tokens.reshape(-1, model_width)
-    gate_part = jnp.dot(flattened[:, :half], gate_own, preferred_element_type=F32) + jnp.dot(
-        flattened[:, half:], gate_other, preferred_element_type=F32
-    )
-    up_part = jnp.dot(flattened[:, :half], up_own, preferred_element_type=F32) + jnp.dot(
-        flattened[:, half:], up_other, preferred_element_type=F32
-    )
-    activation = (jax.nn.silu(gate_part) * up_part).astype(BF16)
-    expert_y = jnp.concatenate(
-        [dot_t(activation, down_own).astype(BF16), dot_t(activation, down_other).astype(BF16)],
-        axis=1,
+    expert_y = experts(
+        flattened, (gate_own, gate_other), (up_own, up_other), (down_own, down_other)
     )
     returned = torus_sum(
         expert_y.reshape(fsdp_count, rows_count * slots_row, model_width),

time: 219 us -> 213 us (0.973)
  matrix products: 13.1 us -> 2.22 us
  Pallas kernels: 151 us -> 157 us
    dot_general x4 -> x0, matrix products: 7.93 us -> none  [the longest x1 3.26 us: local(): jnp.dot(flattened[:, :half], gate_own, preferred_element_type=F32)]
    reshape x3 -> x0, local copies, waits for them, and re-layouts: 5.97 us -> none  [the longest x1 2.26 us: local(): gate_own = gate_own.reshape(-1, units_here)]
    pallas_call x0 -> x2, Pallas kernels: none -> 5.7 us  [the longest x1 3.55 us: experts(): pl.pallas_call(hidden_kernel, out_shape=(part, part), in_specs=[vmem()] *...]
    pad x0 -> x3, local copies, waits for them, and re-layouts: none -> 3.06 us  [widen(): return jnp.pad(values, ((0, 0), (0, 0), (0, units_wide - units_here)))]
    dot_general x3 -> x1, matrix products: 4.06 us -> 1.14 us  [dot_t(): lax.dot_general(left, right, (((1,), (1,)), ((), ())), preferred_element_...]
    unnamed x36 -> x40, local copies, waits for them, and re-layouts: 4.34 us -> 6.6 us
  transfers between devices with their start and end apart: 6 -> 6, of which waited for: 1 -> 1; matrix products, arithmetic and copies ran while one was open for 12% -> 6% of each run, Pallas kernels for 27% -> 29%
where the time goes in v5:
time: 213 us; the launch traced here: 212 us
  Pallas kernels  157 us (74%)
  local copies, waits for them, and re-layouts  20.6 us (10%)
  starting transfers between devices  15.1 us (7%)
  waiting for transfers between devices  10.6 us (5%)
  other arithmetic  6.46 us (3%)
  matrix products  2.22 us (1%)
    pallas_call x4, Pallas kernels, exchange(): pl.pallas_call(functools.partial(exchange_kernel, axis, count, gather, re...  49.1 us
    pallas_call x1, Pallas kernels, prologue(): pl.pallas_call(functools.partial(prologue_kernel, ring, count), out_shape...  35.1 us
    pallas_call x1, Pallas kernels, attention(): pl.pallas_call(functools.partial(attention_kernel, page_len), out_shape=j...  22.8 us
    pallas_call x1, Pallas kernels, torus_gather(): pl.pallas_call(functools.partial(torus_gather_kernel, axis, side), out_sh...  22.4 us
    pallas_call x1, Pallas kernels, torus_sum(): pl.pallas_call(functools.partial(torus_sum_kernel, axis, side), out_shape...  21.8 us
    all_to_all x3, starting transfers between devices, spread_weights(): lax.all_to_all(values, 'dp', split_axis=0, concat_axis=0, tiled=True, axi...  12.9 us
    all_to_all x3, waiting for transfers between devices, spread_weights(): lax.all_to_all(values, 'dp', split_axis=0, concat_axis=0, tiled=True, axi...  10.6 us
    unnamed x40, local copies, waits for them, and re-layouts  6.6 us
  transfers between devices with their start and end apart: 6, of which 1 were waited for; matrix products, arithmetic and copies ran while one was open for 6% of the time, Pallas kernels for 29%

profile of v5, /device:TPU:1, one launch (start us, length us, event | category | flops | bytes accessed | tf_op | source)
XLA Modules:
  0.0 212.4 jit_solution(12275598935501077662)
XLA Ops:
  0.0 1.7 copy.108
  1.7 1.0 pad.10
  2.8 1.0 pad.11
  4.5 35.1 %prologue.1 = (bf16[16,8,2304]{2,1,0:T(8,128)(2,1)}, bf16[4,16,144,128]{3,2,1,0:T(8,128)(2,1)}) custom-call(bf16[8,2304]{1,0:T(8,128)(2,1)} %token_ref.1, bf16[4,144,128]{2,1,0:T(8,128)(2,1)} %pad_maximum_fusion.weight_ref), custom_call_target="tpu_custom_call" | custom-call | tf_op jit(solution)/shard_map/prologue/pallas_call | solution.py:275
  39.6 3.6 %all-to-all-start = ((bf16[8,144,384]{2,1,0:T(8,128)(2,1)}), bf16[8,144,384]{2,1,0:T(8,128)(2,1)S(1)}, u32[]{:S(2)}, u32[]{:S(2)}) async-start(bf16[8,144,384]{2,1,0:T(8,128)(2,1)} %pad.10), calls=%async_computation | async-start | bytes 1769472 | tf_op jit(solution)/shard_map/all_to_all | solution.py:597
  44.7 1.0 fusion.1
  45.7 1.1 select_add_fusion.limit_ref
  46.8 22.8 %attention.1 = bf16[128,128]{1,0:T(8,128)(2,1)} custom-call(bf16[128,2304]{1,0:T(8,128)(2,1)} %bitcast.114, bf16[1,2304]{1,0:T(2,128)(2,1)} %broadcast_in_dim.127.norm_ref, bf16[4,2304,128]{2,1,0:T(8,128)(2,1)} %bitcast.111, f32[128,128]{1,0:T(8,128)} %get-tuple-element.72.cos_ref, f32[128,128]{1,0:T(8,128)} %get-tuple-element.71.sin_ref, ...), custom_call_target="tpu_custom_call" | custom-call | flops 1107296256 | bytes 60000000 | tf_op jit(solution)/shard_map/attention/pallas_call | solution.py:106
  70.3 1.1 slice.117
  72.0 0.9 slice_bitcast_fusion.1
  73.8 12.3 %leaving.1 = bf16[16,1,2432]{2,1,0:T(2,128)(2,1)} custom-call(bf16[16,1,2432]{2,1,0:T(2,128)(2,1)} %copy.69.src_ref), custom_call_target="tpu_custom_call" | custom-call | bytes 200000000 | tf_op jit(solution)/shard_map/leaving/pallas_call | solution.py:187
  86.1 0.9 copy.109
  87.0 5.7 %all-to-all-start.1 = ((bf16[8,144,384]{2,1,0:T(8,128)(2,1)}), bf16[8,144,384]{2,1,0:T(8,128)(2,1)}, u32[]{:S(2)}, u32[]{:S(2)}) async-start(bf16[8,144,384]{2,1,0:T(8,128)(2,1)} %pad.11), calls=%async_computation.1 | async-start | bytes 1769472 | tf_op jit(solution)/shard_map/all_to_all | solution.py:597
  92.9 1.1 fusion.src_ref
  94.1 12.3 %partial_out.1 = f32[8,2304]{1,0:T(8,128)} custom-call(bf16[16,8,2304]{2,1,0:T(8,128)(2,1)} %fusion.src_ref), custom_call_target="tpu_custom_call" | custom-call | bytes 200000000 | tf_op jit(solution)/shard_map/partial_out/pallas_call | solution.py:187
  106.7 1.0 pad.12
  107.9 10.6 %all-to-all-done.1 = bf16[8,144,384]{2,1,0:T(8,128)(2,1)} async-done(((bf16[8,144,384]{2,1,0:T(8,128)(2,1)}), bf16[8,144,384]{2,1,0:T(8,128)(2,1)}, u32[]{:S(2)}, u32[]{:S(2)}) %all-to-all-start.1) | async-done | bytes 884768 | tf_op jit(solution)/shard_map/all_to_all | solution.py:597
  119.2 1.1 slice_reduce_fusion
  121.3 0.9 pad_maximum_fusion.1
  122.2 11.4 %dispatch.1 = bf16[16,2,2304]{2,1,0:T(2,128)(2,1)} custom-call(bf16[16,2,2304]{2,1,0:T(2,128)(2,1)} %bitcast.116), custom_call_target="tpu_custom_call" | custom-call | bytes 200000000 | tf_op jit(solution)/shard_map/dispatch/pallas_call | solution.py:187
  133.6 3.6 %all-to-all-start.2 = ((bf16[8,144,384]{2,1,0:T(8,128)(2,1)}), bf16[8,144,384]{2,1,0:T(8,128)(2,1)S(1)}, u32[]{:S(2)}, u32[]{:S(2)}) async-start(bf16[8,144,384]{2,1,0:T(8,128)(2,1)} %pad.12), calls=%async_computation.2 | async-start | bytes 1769472 | tf_op jit(solution)/shard_map/all_to_all | solution.py:597
  137.9 1.6 reshape.273.src_ref
  139.7 22.4 %expert_tokens.1 = bf16[4,4,32,2304]{3,2,1,0:T(8,128)(2,1)} custom-call(bf16[32,2304]{1,0:T(8,128)(2,1)} %reshape.273.src_ref), custom_call_target="tpu_custom_call" | custom-call | bytes 60000000 | tf_op jit(solution)/shard_map/expert_tokens/pallas_call | solution.py:429
  162.4 0.9 copy-done.2
  163.3 1.7 collective-permute-start.1
  165.3 1.7 copy-done.1
  167.0 1.2 copy-done.3
  168.2 3.5 %experts_hidden.1 = (f32[512,384]{1,0:T(8,128)S(1)}, f32[512,384]{1,0:T(8,128)S(1)}) custom-call(bf16[512,2304]{1,0:T(8,128)(2,1)S(1)} %bitcast.102, bf16[1152,384]{1,0:T(8,128)(2,1)} %bitcast.37.gate_own, bf16[1152,384]{1,0:T(8,128)(2,1)} %collective-permute-done.gate_other, bf16[1152,384]{1,0:T(8,128)(2,1)S(1)} %bitcast.108), custom_call_target="tpu_custom_call" | custom-call | flops 1358954496 | bytes 30000000 | tf_op jit(solution)/shard_map/experts_hidden/pallas_call | solution.py:324
  171.7 2.1 %experts_down.1 = bf16[512,2304]{1,0:T(8,128)(2,1)S(1)} custom-call(bf16[512,2304]{1,0:T(8,128)(2,1)S(1)} %bitcast.103, f32[512,384]{1,0:T(8,128)S(1)} %get-tuple-element.42.gate_ref, f32[512,384]{1,0:T(8,128)S(1)} %get-tuple-element.43.up_ref, bf16[1152,384]{1,0:T(8,128)(2,1)S(1)} %collective-permute-done.1.up_other, bf16[1152,384]{1,0:T(8,128)(2,1)S(1)} %bitcast.106, ...), custom_call_target="tpu_custom_call" | custom-call | tf_op jit(solution)/shard_map/experts_down/pallas_call | solution.py:335
  173.9 21.8 %expert_sums.1 = bf16[32,2304]{1,0:T(8,128)(2,1)S(1)} custom-call(bf16[4,4,32,2304]{3,2,1,0:T(8,128)(2,1)S(1)} %bitcast.104), custom_call_target="tpu_custom_call" | custom-call | tf_op jit(solution)/shard_map/expert_sums/pallas_call | solution.py:541
  196.4 13.1 %back_rows.1 = bf16[16,2,2304]{2,1,0:T(2,128)(2,1)} custom-call(bf16[16,2,2304]{2,1,0:T(2,128)(2,1)} %reshape.278.src_ref), custom_call_target="tpu_custom_call" | custom-call | bytes 200000000 | tf_op jit(solution)/shard_map/back_rows/pallas_call | solution.py:187
  209.6 1.0 fusion.25
  (107 shorter events, 10.5 us)
Async XLA Ops:
  0.0 162.1 %copy-start = (bf16[2304,8]{0,1:T(8,128)(2,1)S(1)}, bf16[2304,8]{0,1:T(8,128)(2,1)}, u32[]{:S(2)}) copy-start(bf16[2304,8]{0,1:T(8,128)(2,1)} %param.21) | copy-start | bytes 110596
  0.0 1.7 copy-start.5
  1.7 2.1 copy-start.8
  1.7 2.1 copy-start.9
  2.8 40.4 %copy-start.16 = (s32[128]{0:T(128)S(1)}, s32[128]{0:T(128)}, u32[]{:S(2)}) copy-start(s32[128]{0:T(128)} %param.27) | copy-start | bytes 1540
  2.8 41.2 %copy-start.12 = (bf16[2304]{0:T(1024)(128)(2,1)S(1)}, bf16[2304]{0:T(1024)(128)(2,1)}, u32[]{:S(2)}) copy-start(bf16[2304]{0:T(1024)(128)(2,1)} %param.19) | copy-start | bytes 13828
  2.8 41.9 %copy-start.14 = (s32[4,4]{1,0:T(4,128)S(1)}, s32[4,4]{1,0:T(4,128)}, u32[]{:S(2)}) copy-start(s32[4,4]{1,0:T(4,128)} %param.25) | copy-start | bytes 196
  2.8 41.9 %copy-start.15 = (s32[128,4]{0,1:T(4,128)S(1)}, s32[128,4]{0,1:T(4,128)}, u32[]{:S(2)}) copy-start(s32[128,4]{0,1:T(4,128)} %param.26) | copy-start | bytes 6148
  39.6 33.4 %all-to-all-start = ((bf16[8,144,384]{2,1,0:T(8,128)(2,1)}), bf16[8,144,384]{2,1,0:T(8,128)(2,1)S(1)}, u32[]{:S(2)}, u32[]{:S(2)}) async-start(bf16[8,144,384]{2,1,0:T(8,128)(2,1)} %pad.10), calls=%async_computation | async-start | bytes 1769472 | tf_op jit(solution)/shard_map/all_to_all | solution.py:597
  46.8 24.6 %copy-start.11 = (s32[8,2]{0,1:T(2,128)S(1)}, s32[8,2]{0,1:T(2,128)}, u32[]{:S(2)}) copy-start(s32[8,2]{0,1:T(2,128)} %param.29) | copy-start | bytes 196
  46.8 24.7 %copy-start.13 = (bf16[2304]{0:T(1024)(128)(2,1)S(1)}, bf16[2304]{0:T(1024)(128)(2,1)}, u32[]{:S(2)}) copy-start(bf16[2304]{0:T(1024)(128)(2,1)} %param.20) | copy-start | bytes 13828
  46.8 24.8 %copy-start.10 = (s32[16,8]{0,1:T(8,128)S(1)}, s32[16,8]{0,1:T(8,128)}, u32[]{:S(2)}) copy-start(s32[16,8]{0,1:T(8,128)} %param.28) | copy-start | bytes 1540
  69.6 23.3 %slice-start = ((bf16[128,128]{1,0:T(8,128)(2,1)}), bf16[120,128]{1,0:T(8,128)(2,1)S(1)}, s32[]{:S(2)}) async-start(bf16[128,128]{1,0:T(8,128)(2,1)} %attention.1), calls=%async_computation.3 | async-start | bytes 61440 | tf_op jit(solution)/shard_map/slice | solution.py:647
  72.0 34.4 %copy-start.4 = (bf16[8,144,2,360]{3,2,1,0:T(2,128)(2,1)S(1)}, bf16[8,144,2,360]{3,2,1,0:T(2,128)(2,1)}, u32[]{:S(2)}) copy-start(bf16[8,144,2,360]{3,2,1,0:T(2,128)(2,1)} %param.22) | copy-start | bytes 4976644
  87.0 31.5 %all-to-all-start.1 = ((bf16[8,144,384]{2,1,0:T(8,128)(2,1)}), bf16[8,144,384]{2,1,0:T(8,128)(2,1)}, u32[]{:S(2)}, u32[]{:S(2)}) async-start(bf16[8,144,384]{2,1,0:T(8,128)(2,1)} %pad.11), calls=%async_computation.1 | async-start | bytes 1769472 | tf_op jit(solution)/shard_map/all_to_all | solution.py:597
  106.6 1.1 copy-start.6
  106.6 1.1 copy-start.7
  133.6 28.7 %all-to-all-start.2 = ((bf16[8,144,384]{2,1,0:T(8,128)(2,1)}), bf16[8,144,384]{2,1,0:T(8,128)(2,1)S(1)}, u32[]{:S(2)}, u32[]{:S(2)}) async-start(bf16[8,144,384]{2,1,0:T(8,128)(2,1)} %pad.12), calls=%async_computation.2 | async-start | bytes 1769472 | tf_op jit(solution)/shard_map/all_to_all | solution.py:597
  137.5 34.2 %collective-permute-start.2 = (bf16[1152,384]{1,0:T(8,128)(2,1)S(1)}, bf16[1152,384]{1,0:T(8,128)(2,1)S(1)}, u32[]{:S(2)}, u32[]{:S(2)}) collective-permute-start(bf16[1152,384]{1,0:T(8,128)(2,1)S(1)} %bitcast.105), channel_id=1, source_target_pairs={{0,16},{16,0},{32,48},{48,32},{64,80},{80,64},{96,112},{112,96},{1... | collective-permute-start | bytes 2654216 | tf_op jit(solution)/shard_map/ppermute | solution.py:641
  139.5 25.8 %collective-permute-start = (bf16[1152,384]{1,0:T(8,128)(2,1)}, bf16[1152,384]{1,0:T(8,128)(2,1)}, u32[]{:S(2)}, u32[]{:S(2)}) collective-permute-start(bf16[1152,384]{1,0:T(8,128)(2,1)} %bitcast.37.gate_own), channel_id=1, source_target_pairs={{0,16},{16,0},{32,48},{48,32},{64,80},{80,64},{96,112},{112,96},{1... | collective-permute-start | bytes 2654216 | tf_op jit(solution)/shard_map/ppermute | solution.py:701
  162.4 0.9 copy-start.2
  163.3 8.4 %collective-permute-start.1 = (bf16[1152,384]{1,0:T(8,128)(2,1)}, bf16[1152,384]{1,0:T(8,128)(2,1)S(1)}, u32[]{:S(2)}, u32[]{:S(2)}) collective-permute-start(bf16[1152,384]{1,0:T(8,128)(2,1)} %bitcast.107), channel_id=1, source_target_pairs={{0,16},{16,0},{32,48},{48,32},{64,80},{80,64},{96,112},{112,96},{1... | collective-permute-start | bytes 2654216 | tf_op jit(solution)/shard_map/ppermute | solution.py:707
  165.3 1.7 copy-start.1
  167.0 1.2 copy-start.3
